TPU v7x, 256 devices: a whole 4x4x8 slice. The times are simulated.
256 devices in a mesh: ball: 16 (over y, x), region: 16 (over z, core).
Axes of the slice: x: 4, y: 4, z: 8, core: 2. Of those that a mesh axis runs over, the one named last changes fastest.
Arguments:
- points: bfloat16 [16, 16, 1024, 256], P('ball', 'region'), may hold values from -6 to 6
- gain_attn: float32 [256], replicated, may hold values from 0.1 to 1.9
- w_query_key: bfloat16 [256, 512], replicated, may hold values from -7 to 7
- w_value: bfloat16 [256, 256], replicated, may hold values from -0.375 to 0.375
- w_out: bfloat16 [256, 256], replicated, may hold values from -0.375 to 0.375
- gain_mlp: float32 [256], replicated, may hold values from 0.1 to 1.9
- w_up: bfloat16 [256, 1024], replicated, may hold values from -0.375 to 0.375
- w_down: bfloat16 [1024, 256], replicated, may hold values from -0.1875 to 0.1875
- cluster_dest: int32 [16, 16, 16], P('ball', 'region'), may hold values from 0 to 255, as said below
Outputs:
- block_out: bfloat16 [16, 16, 1024, 256], P('ball', 'region')
Inputs may be any that keep to these rules, and one draw needn't show every extreme that they name: cluster_dest[l, r, c] = o * 16 + s sends cluster c of lane l, region r to slot s of lane o, region r. Within one region all values are distinct. Each lane sends exactly 2 clusters to each of 8 owner lanes and none to the others, and the offsets (o - l) mod 16 of those owners are the same set for every lane of one region.
All inputs are finite; a program needn't handle non-finite values.
Results may differ from a plain program's by a relative error of at most 0.012.
The roundings to bfloat16 on the way count: a program that leaves them out, or rounds other values in their place, can miss the bound.
Values may be sent and summed in bfloat16 or wider, within the bound.
A program may use at most 64 MiB of HBM per device.

v0:
```python
import math

import jax
import jax.numpy as jnp
from jax import lax
from jax.sharding import PartitionSpec as P

HEADS = 8
BALL = 1024
CLUSTER = 64
POOL = 16


def gather_turned(arrays, axis, dims):
    turned = [jnp.moveaxis(a, dim, 0) for a, dim in zip(arrays, dims)]
    widths = [t[0].size for t in turned]
    both = jnp.concatenate([t.reshape(-1, w) for t, w in zip(turned, widths)], axis=1)
    whole = lax.all_gather(both, axis, axis=0, tiled=True)
    blocks = jnp.split(whole, [sum(widths[:k]) for k in range(1, len(widths))], axis=1)
    return tuple(
        (
            jnp.moveaxis(b.reshape(-1, *t.shape[1:]), 0, dim)
            for b, t, dim in zip(blocks, turned, dims)
        )
    )


def rms_norm(row_data, gain_vector):
    widened = row_data.astype(jnp.float32)
    scaling = lax.rsqrt(jnp.mean(widened * widened, axis=1, keepdims=True) + 1e-06)
    return (widened * scaling * gain_vector).astype(jnp.bfloat16)


def attend_columns(query_cols, key_parts, value_parts):
    columns, row_count = query_cols.shape
    head_size = columns // HEADS
    query_heads = query_cols.reshape(HEADS, head_size, row_count)
    key_heads = tuple((part.reshape(HEADS, head_size, part.shape[1]) for part in key_parts))
    value_heads = tuple((part.reshape(HEADS, head_size, part.shape[1]) for part in value_parts))
    scale = 1.0 / math.sqrt(head_size)

    def one_head(operands):
        query_head, key_list, value_list = operands
        scores = [
            jnp.einsum("dn,dm->nm", query_head, key_head, preferred_element_type=jnp.float32)
            * scale
            for key_head in key_list
        ]
        row_max = scores[0].max(axis=1, keepdims=True)
        for extra in scores[1:]:
            row_max = jnp.maximum(row_max, extra.max(axis=1, keepdims=True))
        exponents = [jnp.exp(block - row_max) for block in scores]
        total = exponents[0].sum(axis=1, keepdims=True)
        for extra in exponents[1:]:
            total = total + extra.sum(axis=1, keepdims=True)
        mixed = jnp.zeros((head_size, row_count), jnp.float32)
        for exponent, value_head in zip(exponents, value_list):
            weights = (exponent / total).astype(jnp.bfloat16)
            mixed = mixed + jnp.einsum(
                "nm,dm->dn", weights, value_head, preferred_element_type=jnp.float32
            )
        return mixed.astype(jnp.bfloat16)

    result = lax.map(one_head, (query_heads, key_heads, value_heads))
    return result.reshape(columns, row_count)


def per_device(
    points, gain_attn, w_query_key, w_value, w_out, gain_mlp, w_up, w_down, cluster_dest
):
    columns = points.shape[-1]
    flat = points.reshape(-1, columns)
    row_count = flat.shape[0]
    lanes = lax.axis_size("ball")
    clusters = row_count // CLUSTER
    capacity = 2 * clusters // lanes
    ball_count = row_count // BALL
    ball_ids = jnp.arange(ball_count, dtype=jnp.int32)

    def project(states):
        paired = jnp.dot(states, w_query_key, preferred_element_type=jnp.float32).astype(
            jnp.bfloat16
        )
        projected = jnp.dot(states, w_value, preferred_element_type=jnp.float32).astype(
            jnp.bfloat16
        )
        return (paired[:, :columns], paired[:, columns:], projected)

    normed = rms_norm(flat, gain_attn)
    query, keys, values = project(normed)
    query_cols, key_cols, value_cols = (query.T, keys.T, values.T)

    def pooled(source_cols):
        summed = jnp.sum(source_cols.reshape(columns, -1, POOL), axis=2, dtype=jnp.float32)
        return (summed / math.sqrt(POOL)).astype(jnp.bfloat16)

    gathered_keys, gathered_values = gather_turned(
        (pooled(key_cols), pooled(value_cols)), "region", (1, 1)
    )

    def near_ball(index):
        return attend_columns(query_cols, (key_cols, gathered_keys), (value_cols, gathered_values))

    near = lax.map(near_ball, ball_ids)
    near_out = jnp.einsum("bcn,cf->bnf", near, w_out, preferred_element_type=jnp.float32).reshape(
        row_count, columns
    )
    targets = cluster_dest.reshape(-1)
    owner = targets // clusters
    slot = targets % clusters
    cluster_ids = jnp.arange(clusters, dtype=jnp.int32)
    earlier = (owner[:, None] == owner[None, :]) & (cluster_ids[None, :] < cluster_ids[:, None])
    rank = jnp.sum(earlier.astype(jnp.int32), axis=1)
    position = owner * capacity + rank
    placing = jnp.arange(lanes * capacity, dtype=jnp.int32)[:, None] == position[None, :]
    place_matrix = placing.astype(jnp.bfloat16)
    sent_ids = jnp.max(jnp.where(placing, slot[None, :], -1), axis=1).reshape(lanes, capacity)
    inner = normed.shape[1]
    packed = jnp.dot(
        place_matrix, normed.reshape(clusters, CLUSTER * inner), preferred_element_type=jnp.float32
    )
    got_states = lax.all_to_all(
        packed.astype(jnp.bfloat16).reshape(lanes, capacity * CLUSTER, inner),
        "ball",
        split_axis=0,
        concat_axis=0,
        tiled=True,
    )
    got_ids = lax.all_to_all(sent_ids, "ball", split_axis=0, concat_axis=0, tiled=True)
    fill_matrix = (cluster_ids[:, None] == got_ids.reshape(1, -1)).astype(jnp.bfloat16)
    inner = got_states.shape[2]
    settled = jnp.dot(
        fill_matrix,
        got_states.reshape(lanes * capacity, CLUSTER * inner),
        preferred_element_type=jnp.float32,
    )
    rotated_query, rotated_keys, rotated_values = project(
        settled.astype(jnp.bfloat16).reshape(row_count, inner)
    )
    rot_query_cols, rot_key_cols, rot_value_cols = (
        rotated_query.T,
        rotated_keys.T,
        rotated_values.T,
    )

    def far_ball(index):
        return attend_columns(rot_query_cols, (rot_key_cols,), (rot_value_cols,))

    far_rotated = lax.map(far_ball, ball_ids).transpose(0, 2, 1).reshape(row_count, columns)
    outgoing = jnp.einsum(
        "sk,sw->kw",
        fill_matrix,
        far_rotated.reshape(clusters, CLUSTER * columns),
        preferred_element_type=jnp.float32,
    )
    outgoing = outgoing.astype(jnp.bfloat16).reshape(lanes, capacity * CLUSTER, columns)
    returned = lax.all_to_all(outgoing, "ball", split_axis=0, concat_axis=0, tiled=True)
    far = jnp.einsum(
        "kc,kw->cw",
        place_matrix,
        returned.reshape(lanes * capacity, CLUSTER * columns),
        preferred_element_type=jnp.float32,
    )
    far = far.astype(jnp.bfloat16).reshape(row_count, columns)
    after = (
        flat.astype(jnp.float32)
        + near_out
        + jnp.dot(far, w_out, preferred_element_type=jnp.float32)
    ).astype(jnp.bfloat16)
    normed_mlp = rms_norm(after, gain_mlp)
    hidden = jax.nn.gelu(
        jnp.dot(normed_mlp, w_up, preferred_element_type=jnp.float32), approximate=True
    ).astype(jnp.bfloat16)
    block_out = (
        after.astype(jnp.float32) + jnp.dot(hidden, w_down, preferred_element_type=jnp.float32)
    ).astype(jnp.bfloat16)
    return block_out.reshape(points.shape)


def solution(mesh):
    placed = (
        P("ball", "region", None, None),
        P(),
        P(),
        P(),
        P(),
        P(),
        P(),
        P(),
        P("ball", "region", None),
    )
    return jax.shard_map(
        per_device,
        mesh=mesh,
        in_specs=placed,
        out_specs=P("ball", "region", None, None),
        check_vma=False,
    )
```

profile of v0, /device:TPU:1, one launch (start us, length us, event | category | flops | bytes accessed | tf_op | source)
XLA Modules:
  0.0 153.3 jit_solution(158105312404445815)
XLA Ops:
  8.2 7.6 %all-to-all-start = ((s32[16,1,2]{2,1,0:T(1,128)}), s32[16,1,2]{2,1,0:T(1,128)S(1)}, u32[]{:S(2)}, u32[]{:S(2)}) async-start(s32[16,1,2]{2,1,0:T(1,128)} %bitcast.27), calls=%async_computation | async-start | bytes 16384 | tf_op jit(solution)/shard_map/all_to_all | solution.py:129
  15.8 1.3 copy.41
  18.3 1.2 reshape.241
  19.6 2.8 %convolution_convert_fusion.1 = bf16[32,16384]{1,0:T(8,128)(2,1)} fusion(f32[16,16384]{1,0:T(8,128)} %reshape.241, f32[16,16384]{1,0:T(8,128)S(1)} %bitcast.159, f32[16384]{0:T(1024)S(1)} %bitcast.173, s32[16]{0:T(128)S(1)} %multiply_add_fusion), kind=kOutput, calls=%fused_computation.53 | convolution fusion | flops 18088448 | bytes 3211328 | tf_op jit(solution)/shard_map/dot_general | solution.py:119
  22.9 2.4 %reshape.228 = bf16[16,128,256]{2,1,0:T(8,128)(2,1)} reshape(bf16[32,16384]{1,0:T(8,128)(2,1)} %convolution_convert_fusion.1) | data formatting | bytes 2097152 | tf_op jit(solution)/shard_map/reshape | solution.py:123
  25.3 6.8 %all-to-all-start.1 = ((bf16[16,128,256]{2,1,0:T(8,128)(2,1)}), bf16[16,128,256]{2,1,0:T(8,128)(2,1)}, u32[]{:S(2)}, u32[]{:S(2)}) async-start(bf16[16,128,256]{2,1,0:T(8,128)(2,1)} %reshape.228), calls=%async_computation.1 | async-start | bytes 2097152 | tf_op jit(solution)/shard_map/all_to_all | solution.py:122
  37.3 10.4 %all-to-all-done.1 = bf16[16,128,256]{2,1,0:T(8,128)(2,1)} async-done(((bf16[16,128,256]{2,1,0:T(8,128)(2,1)}), bf16[16,128,256]{2,1,0:T(8,128)(2,1)}, u32[]{:S(2)}, u32[]{:S(2)}) %all-to-all-start.1) | async-done | bytes 1048608 | tf_op jit(solution)/shard_map/all_to_all | solution.py:122
  47.7 1.6 %reshape.229 = bf16[32,16384]{1,0:T(8,128)(2,1)S(1)} reshape(bf16[16,128,256]{2,1,0:T(8,128)(2,1)} %all-to-all-done.1) | data formatting | bytes 2097152 | tf_op jit(solution)/shard_map/reshape | solution.py:134
  50.8 19.3 %while.35 = (s32[]{:T(128)}, bf16[8,32,1024]{2,1,0:T(8,128)(2,1)S(1)}, bf16[8,32,1024]{2,1,0:T(8,128)(2,1)S(1)}, bf16[8,32,1024]{2,1,0:T(8,128)(2,1)S(1)}, bf16[8,32,1024]{2,1,0:T(8,128)(2,1)S(1)}, /*index=5*/s32[]{:T(128)}) while((s32[]{:T(128)}, bf16[8,32,1024]{2,1,0:T(8,128)(2,1)S(1)}, bf16[8,32,1024]{2,1,0:T(8,128)(2,1)S(1)}, ...), condition=%wide.region_14.15_spmd, body=%wide.region_11.14_spmd.sunk | while | flops 143685632 | bytes 12867653 | solution.py:64
  71.0 1.3 reshape.234
  72.4 4.4 %all-to-all-start.2 = ((bf16[16,128,256]{2,1,0:T(8,128)(2,1)}), bf16[16,128,256]{2,1,0:T(8,128)(2,1)S(1)}, u32[]{:S(2)}, u32[]{:S(2)}) async-start(bf16[16,128,256]{2,1,0:T(8,128)(2,1)} %reshape.234), calls=%async_computation.2 | async-start | bytes 2097152 | tf_op jit(solution)/shard_map/all_to_all | solution.py:157
  76.8 1.3 all-gather.2.cloned.1.call-done
  78.1 1.3 fusion.82
  80.6 59.0 %while.34 = (s32[]{:T(128)}, bf16[8,32,1024]{2,1,0:T(8,128)(2,1)S(1)}, bf16[8,32,1024]{2,1,0:T(8,128)(2,1)}, bf16[8,32,1024]{2,1,0:T(8,128)(2,1)}, bf16[8,32,102...) while((s32[]{:T(128)}, ...), condition=%wide.region_8.9_spmd, body=%wide.region_3.8_spmd.sunk | while | flops 287373312 | bytes 25951828 | solution.py:64
  80.7 1.6 %multiply_reduce_fusion.6 = (f32[1024]{0:T(1024)S(1)}, f32[1024,1024]{0,1:T(8,128)S(1)}) fusion(bf16[8,32,1024]{2,1,0:T(8,128)(2,1)} %get-tuple-element.278, s32[]{:T(128)} %get-tuple-element.266, bf16[8,32,1024]{2,1,0:T(8,128)(2,1)} %get-tuple-element.277), kind=kOutput, calls=%fused_computation.5.clone.1 | convolution fusion | flops 69204992 | bytes 4330496 | tf_op jit(solution)/shard_map/while/body/eval_jaxpr/while/body/eval_jaxpr/dn,dm->nm/dot_general | solution.py:45
  82.3 1.6 %multiply_reduce_fusion.7 = (f32[1024]{0:T(1024)S(1)}, f32[1024,1024]{0,1:T(8,128)S(1)}) fusion(bf16[8,32,1024]{2,1,0:T(8,128)(2,1)} %get-tuple-element.279, s32[]{:T(128)} %get-tuple-element.266, bf16[8,32,1024]{2,1,0:T(8,128)(2,1)} %get-tuple-element.277), kind=kOutput, calls=%fused_computation.4.clone.1 | convolution fusion | flops 69204992 | bytes 4330496 | tf_op jit(solution)/shard_map/while/body/eval_jaxpr/while/body/eval_jaxpr/dn,dm->nm/dot_general | solution.py:45
  84.0 1.4 fusion.108
  85.3 1.7 %fusion.109 = f32[32,1024]{1,0:T(8,128)S(1)} fusion(f32[1024,1024]{0,1:T(8,128)S(1)} %get-tuple-element.245, f32[1024]{0:T(1024)S(1)} %add.171, f32[1024]{0:T(1024)S(1)} %max.9, bf16[8,32,1024]{2,1,0:T(8,128)(2,1)} %get-tuple-element.276, s32[]{:T(128)} %get-tuple-element.266), kind=kOutput, calls=%fused_computation.8.clone.1 | convolution fusion | flops 71303168 | bytes 4399616 | tf_op jit(solution)/shard_map/while/body/eval_jaxpr/while/body/eval_jaxpr/nm,dm->dn/dot_general | solution.py:59
  88.0 1.6 %multiply_reduce_fusion.6 = (f32[1024]{0:T(1024)S(1)}, f32[1024,1024]{0,1:T(8,128)S(1)}) fusion(bf16[8,32,1024]{2,1,0:T(8,128)(2,1)} %get-tuple-element.278, s32[]{:T(128)} %get-tuple-element.266, bf16[8,32,1024]{2,1,0:T(8,128)(2,1)} %get-tuple-element.277), kind=kOutput, calls=%fused_computation.5.clone.1 | convolution fusion | flops 69204992 | bytes 4330496 | tf_op jit(solution)/shard_map/while/body/eval_jaxpr/while/body/eval_jaxpr/dn,dm->nm/dot_general | solution.py:45
  89.7 1.6 %multiply_reduce_fusion.7 = (f32[1024]{0:T(1024)S(1)}, f32[1024,1024]{0,1:T(8,128)S(1)}) fusion(bf16[8,32,1024]{2,1,0:T(8,128)(2,1)} %get-tuple-element.279, s32[]{:T(128)} %get-tuple-element.266, bf16[8,32,1024]{2,1,0:T(8,128)(2,1)} %get-tuple-element.277), kind=kOutput, calls=%fused_computation.4.clone.1 | convolution fusion | flops 69204992 | bytes 4330496 | tf_op jit(solution)/shard_map/while/body/eval_jaxpr/while/body/eval_jaxpr/dn,dm->nm/dot_general | solution.py:45
  91.3 1.4 fusion.108
  92.7 1.7 %fusion.109 = f32[32,1024]{1,0:T(8,128)S(1)} fusion(f32[1024,1024]{0,1:T(8,128)S(1)} %get-tuple-element.245, f32[1024]{0:T(1024)S(1)} %add.171, f32[1024]{0:T(1024)S(1)} %max.9, bf16[8,32,1024]{2,1,0:T(8,128)(2,1)} %get-tuple-element.276, s32[]{:T(128)} %get-tuple-element.266), kind=kOutput, calls=%fused_computation.8.clone.1 | convolution fusion | flops 71303168 | bytes 4399616 | tf_op jit(solution)/shard_map/while/body/eval_jaxpr/while/body/eval_jaxpr/nm,dm->dn/dot_general | solution.py:59
  95.4 1.6 %multiply_reduce_fusion.6 = (f32[1024]{0:T(1024)S(1)}, f32[1024,1024]{0,1:T(8,128)S(1)}) fusion(bf16[8,32,1024]{2,1,0:T(8,128)(2,1)} %get-tuple-element.278, s32[]{:T(128)} %get-tuple-element.266, bf16[8,32,1024]{2,1,0:T(8,128)(2,1)} %get-tuple-element.277), kind=kOutput, calls=%fused_computation.5.clone.1 | convolution fusion | flops 69204992 | bytes 4330496 | tf_op jit(solution)/shard_map/while/body/eval_jaxpr/while/body/eval_jaxpr/dn,dm->nm/dot_general | solution.py:45
  97.1 1.6 %multiply_reduce_fusion.7 = (f32[1024]{0:T(1024)S(1)}, f32[1024,1024]{0,1:T(8,128)S(1)}) fusion(bf16[8,32,1024]{2,1,0:T(8,128)(2,1)} %get-tuple-element.279, s32[]{:T(128)} %get-tuple-element.266, bf16[8,32,1024]{2,1,0:T(8,128)(2,1)} %get-tuple-element.277), kind=kOutput, calls=%fused_computation.4.clone.1 | convolution fusion | flops 69204992 | bytes 4330496 | tf_op jit(solution)/shard_map/while/body/eval_jaxpr/while/body/eval_jaxpr/dn,dm->nm/dot_general | solution.py:45
  98.7 1.4 fusion.108
  100.1 1.7 %fusion.109 = f32[32,1024]{1,0:T(8,128)S(1)} fusion(f32[1024,1024]{0,1:T(8,128)S(1)} %get-tuple-element.245, f32[1024]{0:T(1024)S(1)} %add.171, f32[1024]{0:T(1024)S(1)} %max.9, bf16[8,32,1024]{2,1,0:T(8,128)(2,1)} %get-tuple-element.276, s32[]{:T(128)} %get-tuple-element.266), kind=kOutput, calls=%fused_computation.8.clone.1 | convolution fusion | flops 71303168 | bytes 4399616 | tf_op jit(solution)/shard_map/while/body/eval_jaxpr/while/body/eval_jaxpr/nm,dm->dn/dot_general | solution.py:59
  102.8 1.6 %multiply_reduce_fusion.6 = (f32[1024]{0:T(1024)S(1)}, f32[1024,1024]{0,1:T(8,128)S(1)}) fusion(bf16[8,32,1024]{2,1,0:T(8,128)(2,1)} %get-tuple-element.278, s32[]{:T(128)} %get-tuple-element.266, bf16[8,32,1024]{2,1,0:T(8,128)(2,1)} %get-tuple-element.277), kind=kOutput, calls=%fused_computation.5.clone.1 | convolution fusion | flops 69204992 | bytes 4330496 | tf_op jit(solution)/shard_map/while/body/eval_jaxpr/while/body/eval_jaxpr/dn,dm->nm/dot_general | solution.py:45
  104.4 1.6 %multiply_reduce_fusion.7 = (f32[1024]{0:T(1024)S(1)}, f32[1024,1024]{0,1:T(8,128)S(1)}) fusion(bf16[8,32,1024]{2,1,0:T(8,128)(2,1)} %get-tuple-element.279, s32[]{:T(128)} %get-tuple-element.266, bf16[8,32,1024]{2,1,0:T(8,128)(2,1)} %get-tuple-element.277), kind=kOutput, calls=%fused_computation.4.clone.1 | convolution fusion | flops 69204992 | bytes 4330496 | tf_op jit(solution)/shard_map/while/body/eval_jaxpr/while/body/eval_jaxpr/dn,dm->nm/dot_general | solution.py:45
  106.1 1.4 fusion.108
  107.5 1.7 %fusion.109 = f32[32,1024]{1,0:T(8,128)S(1)} fusion(f32[1024,1024]{0,1:T(8,128)S(1)} %get-tuple-element.245, f32[1024]{0:T(1024)S(1)} %add.171, f32[1024]{0:T(1024)S(1)} %max.9, bf16[8,32,1024]{2,1,0:T(8,128)(2,1)} %get-tuple-element.276, s32[]{:T(128)} %get-tuple-element.266), kind=kOutput, calls=%fused_computation.8.clone.1 | convolution fusion | flops 71303168 | bytes 4399616 | tf_op jit(solution)/shard_map/while/body/eval_jaxpr/while/body/eval_jaxpr/nm,dm->dn/dot_general | solution.py:59
  110.2 1.6 %multiply_reduce_fusion.6 = (f32[1024]{0:T(1024)S(1)}, f32[1024,1024]{0,1:T(8,128)S(1)}) fusion(bf16[8,32,1024]{2,1,0:T(8,128)(2,1)} %get-tuple-element.278, s32[]{:T(128)} %get-tuple-element.266, bf16[8,32,1024]{2,1,0:T(8,128)(2,1)} %get-tuple-element.277), kind=kOutput, calls=%fused_computation.5.clone.1 | convolution fusion | flops 69204992 | bytes 4330496 | tf_op jit(solution)/shard_map/while/body/eval_jaxpr/while/body/eval_jaxpr/dn,dm->nm/dot_general | solution.py:45
  111.8 1.6 %multiply_reduce_fusion.7 = (f32[1024]{0:T(1024)S(1)}, f32[1024,1024]{0,1:T(8,128)S(1)}) fusion(bf16[8,32,1024]{2,1,0:T(8,128)(2,1)} %get-tuple-element.279, s32[]{:T(128)} %get-tuple-element.266, bf16[8,32,1024]{2,1,0:T(8,128)(2,1)} %get-tuple-element.277), kind=kOutput, calls=%fused_computation.4.clone.1 | convolution fusion | flops 69204992 | bytes 4330496 | tf_op jit(solution)/shard_map/while/body/eval_jaxpr/while/body/eval_jaxpr/dn,dm->nm/dot_general | solution.py:45
  113.5 1.4 fusion.108
  114.9 1.7 %fusion.109 = f32[32,1024]{1,0:T(8,128)S(1)} fusion(f32[1024,1024]{0,1:T(8,128)S(1)} %get-tuple-element.245, f32[1024]{0:T(1024)S(1)} %add.171, f32[1024]{0:T(1024)S(1)} %max.9, bf16[8,32,1024]{2,1,0:T(8,128)(2,1)} %get-tuple-element.276, s32[]{:T(128)} %get-tuple-element.266), kind=kOutput, calls=%fused_computation.8.clone.1 | convolution fusion | flops 71303168 | bytes 4399616 | tf_op jit(solution)/shard_map/while/body/eval_jaxpr/while/body/eval_jaxpr/nm,dm->dn/dot_general | solution.py:59
  117.5 1.6 %multiply_reduce_fusion.6 = (f32[1024]{0:T(1024)S(1)}, f32[1024,1024]{0,1:T(8,128)S(1)}) fusion(bf16[8,32,1024]{2,1,0:T(8,128)(2,1)} %get-tuple-element.278, s32[]{:T(128)} %get-tuple-element.266, bf16[8,32,1024]{2,1,0:T(8,128)(2,1)} %get-tuple-element.277), kind=kOutput, calls=%fused_computation.5.clone.1 | convolution fusion | flops 69204992 | bytes 4330496 | tf_op jit(solution)/shard_map/while/body/eval_jaxpr/while/body/eval_jaxpr/dn,dm->nm/dot_general | solution.py:45
  119.2 1.6 %multiply_reduce_fusion.7 = (f32[1024]{0:T(1024)S(1)}, f32[1024,1024]{0,1:T(8,128)S(1)}) fusion(bf16[8,32,1024]{2,1,0:T(8,128)(2,1)} %get-tuple-element.279, s32[]{:T(128)} %get-tuple-element.266, bf16[8,32,1024]{2,1,0:T(8,128)(2,1)} %get-tuple-element.277), kind=kOutput, calls=%fused_computation.4.clone.1 | convolution fusion | flops 69204992 | bytes 4330496 | tf_op jit(solution)/shard_map/while/body/eval_jaxpr/while/body/eval_jaxpr/dn,dm->nm/dot_general | solution.py:45
  120.8 1.4 fusion.108
  122.2 1.7 %fusion.109 = f32[32,1024]{1,0:T(8,128)S(1)} fusion(f32[1024,1024]{0,1:T(8,128)S(1)} %get-tuple-element.245, f32[1024]{0:T(1024)S(1)} %add.171, f32[1024]{0:T(1024)S(1)} %max.9, bf16[8,32,1024]{2,1,0:T(8,128)(2,1)} %get-tuple-element.276, s32[]{:T(128)} %get-tuple-element.266), kind=kOutput, calls=%fused_computation.8.clone.1 | convolution fusion | flops 71303168 | bytes 4399616 | tf_op jit(solution)/shard_map/while/body/eval_jaxpr/while/body/eval_jaxpr/nm,dm->dn/dot_general | solution.py:59
  124.9 1.6 %multiply_reduce_fusion.6 = (f32[1024]{0:T(1024)S(1)}, f32[1024,1024]{0,1:T(8,128)S(1)}) fusion(bf16[8,32,1024]{2,1,0:T(8,128)(2,1)} %get-tuple-element.278, s32[]{:T(128)} %get-tuple-element.266, bf16[8,32,1024]{2,1,0:T(8,128)(2,1)} %get-tuple-element.277), kind=kOutput, calls=%fused_computation.5.clone.1 | convolution fusion | flops 69204992 | bytes 4330496 | tf_op jit(solution)/shard_map/while/body/eval_jaxpr/while/body/eval_jaxpr/dn,dm->nm/dot_general | solution.py:45
  126.6 1.6 %multiply_reduce_fusion.7 = (f32[1024]{0:T(1024)S(1)}, f32[1024,1024]{0,1:T(8,128)S(1)}) fusion(bf16[8,32,1024]{2,1,0:T(8,128)(2,1)} %get-tuple-element.279, s32[]{:T(128)} %get-tuple-element.266, bf16[8,32,1024]{2,1,0:T(8,128)(2,1)} %get-tuple-element.277), kind=kOutput, calls=%fused_computation.4.clone.1 | convolution fusion | flops 69204992 | bytes 4330496 | tf_op jit(solution)/shard_map/while/body/eval_jaxpr/while/body/eval_jaxpr/dn,dm->nm/dot_general | solution.py:45
  128.2 1.4 fusion.108
  129.6 1.7 %fusion.109 = f32[32,1024]{1,0:T(8,128)S(1)} fusion(f32[1024,1024]{0,1:T(8,128)S(1)} %get-tuple-element.245, f32[1024]{0:T(1024)S(1)} %add.171, f32[1024]{0:T(1024)S(1)} %max.9, bf16[8,32,1024]{2,1,0:T(8,128)(2,1)} %get-tuple-element.276, s32[]{:T(128)} %get-tuple-element.266), kind=kOutput, calls=%fused_computation.8.clone.1 | convolution fusion | flops 71303168 | bytes 4399616 | tf_op jit(solution)/shard_map/while/body/eval_jaxpr/while/body/eval_jaxpr/nm,dm->dn/dot_general | solution.py:59
  132.3 1.6 %multiply_reduce_fusion.6 = (f32[1024]{0:T(1024)S(1)}, f32[1024,1024]{0,1:T(8,128)S(1)}) fusion(bf16[8,32,1024]{2,1,0:T(8,128)(2,1)} %get-tuple-element.278, s32[]{:T(128)} %get-tuple-element.266, bf16[8,32,1024]{2,1,0:T(8,128)(2,1)} %get-tuple-element.277), kind=kOutput, calls=%fused_computation.5.clone.1 | convolution fusion | flops 69204992 | bytes 4330496 | tf_op jit(solution)/shard_map/while/body/eval_jaxpr/while/body/eval_jaxpr/dn,dm->nm/dot_general | solution.py:45
  133.9 1.6 %multiply_reduce_fusion.7 = (f32[1024]{0:T(1024)S(1)}, f32[1024,1024]{0,1:T(8,128)S(1)}) fusion(bf16[8,32,1024]{2,1,0:T(8,128)(2,1)} %get-tuple-element.279, s32[]{:T(128)} %get-tuple-element.266, bf16[8,32,1024]{2,1,0:T(8,128)(2,1)} %get-tuple-element.277), kind=kOutput, calls=%fused_computation.4.clone.1 | convolution fusion | flops 69204992 | bytes 4330496 | tf_op jit(solution)/shard_map/while/body/eval_jaxpr/while/body/eval_jaxpr/dn,dm->nm/dot_general | solution.py:45
  135.6 1.4 fusion.108
  137.0 1.7 %fusion.109 = f32[32,1024]{1,0:T(8,128)S(1)} fusion(f32[1024,1024]{0,1:T(8,128)S(1)} %get-tuple-element.245, f32[1024]{0:T(1024)S(1)} %add.171, f32[1024]{0:T(1024)S(1)} %max.9, bf16[8,32,1024]{2,1,0:T(8,128)(2,1)} %get-tuple-element.276, s32[]{:T(128)} %get-tuple-element.266), kind=kOutput, calls=%fused_computation.8.clone.1 | convolution fusion | flops 71303168 | bytes 4399616 | tf_op jit(solution)/shard_map/while/body/eval_jaxpr/while/body/eval_jaxpr/nm,dm->dn/dot_general | solution.py:59
  141.6 1.4 convolution_add_fusion.1
  143.4 2.0 %fusion.54 = bf16[1,1,1024,256]{2,3,1,0:T(8,128)(2,1)S(1)} fusion(bf16[1024,256]{1,0:T(8,128)(2,1)S(1)} %copy-done, bf16[256,1024]{1,0:T(8,128)(2,1)S(1)} %copy-done.8, bf16[1024,256]{0,1:T(8,128)(2,1)S(1)} %get-tuple-element.165, f32[256]{0:T(256)S(1)} %copy-done.9, f32[1024]{0:T(1024)S(1)} %add_rsqrt_fusion), kind=kOutput, calls=%fused_computation.77 | convolution fusion | flops 1085014016 | bytes 2102272 | tf_op jit(solution)/shard_map/dot_general | solution.py:175
  (114 shorter events, 42.2 us)
Async XLA Ops:
  6.5 136.9 %copy-start = (bf16[1024,256]{1,0:T(8,128)(2,1)S(1)}, bf16[1024,256]{1,0:T(8,128)(2,1)}, u32[]{:S(2)}) copy-start(bf16[1024,256]{1,0:T(8,128)(2,1)} %param.20) | copy-start | bytes 1572868
  7.5 12.2 %copy-start.6 = (s32[16]{0:T(128)}, s32[16]{0:T(128)S(1)}, u32[]{:S(2)}) copy-start(s32[16]{0:T(128)S(1)} %multiply_add_fusion) | copy-start | bytes 196
  8.2 17.0 %all-to-all-start = ((s32[16,1,2]{2,1,0:T(1,128)}), s32[16,1,2]{2,1,0:T(1,128)S(1)}, u32[]{:S(2)}, u32[]{:S(2)}) async-start(s32[16,1,2]{2,1,0:T(1,128)} %bitcast.27), calls=%async_computation | async-start | bytes 16384 | tf_op jit(solution)/shard_map/all_to_all | solution.py:129
  15.8 3.7 %copy-start.5 = (f32[256]{0:T(256)S(1)}, f32[256]{0:T(256)}, u32[]{:S(2)}) copy-start(f32[256]{0:T(256)} %param.14) | copy-start | bytes 3076
  17.5 4.9 %copy-start.2 = (bf16[256,512]{1,0:T(8,128)(2,1)S(1)}, bf16[256,512]{1,0:T(8,128)(2,1)}, u32[]{:S(2)}) copy-start(bf16[256,512]{1,0:T(8,128)(2,1)} %param.15) | copy-start | bytes 786436
  25.3 8.6 %copy-start.4 = (bf16[256,256]{1,0:T(8,128)(2,1)S(1)}, bf16[256,256]{1,0:T(8,128)(2,1)}, u32[]{:S(2)}) copy-start(bf16[256,256]{1,0:T(8,128)(2,1)} %param.16) | copy-start | bytes 393220
  25.3 22.4 %all-to-all-start.1 = ((bf16[16,128,256]{2,1,0:T(8,128)(2,1)}), bf16[16,128,256]{2,1,0:T(8,128)(2,1)}, u32[]{:S(2)}, u32[]{:S(2)}) async-start(bf16[16,128,256]{2,1,0:T(8,128)(2,1)} %reshape.228), calls=%async_computation.1 | async-start | bytes 2097152 | tf_op jit(solution)/shard_map/all_to_all | solution.py:122
  32.1 46.0 %all-gather.2.cloned.1.call-start = ((), (), s32[]{:S(2)}) async-start(), calls=%async_computation.3 | async-start | bytes 1114112 | tf_op jit(solution)/shard_map/all_gather | solution.py:18
  72.4 68.1 %all-to-all-start.2 = ((bf16[16,128,256]{2,1,0:T(8,128)(2,1)}), bf16[16,128,256]{2,1,0:T(8,128)(2,1)S(1)}, u32[]{:S(2)}, u32[]{:S(2)}) async-start(bf16[16,128,256]{2,1,0:T(8,128)(2,1)} %reshape.234), calls=%async_computation.2 | async-start | bytes 2097152 | tf_op jit(solution)/shard_map/all_to_all | solution.py:157
  80.6 60.4 %copy-start.7 = (s32[16]{0:T(128)S(1)}, s32[16]{0:T(128)}, u32[]{:S(2)}) copy-start(s32[16]{0:T(128)} %copy-done.6) | copy-start | bytes 196
  139.7 0.8 copy-start.1
  140.5 1.2 copy-start.3
  140.5 2.9 %copy-start.9 = (f32[256]{0:T(256)S(1)}, f32[256]{0:T(256)}, u32[]{:S(2)}) copy-start(f32[256]{0:T(256)} %param.18) | copy-start | bytes 3076
  141.4 2.1 %copy-start.8 = (bf16[256,1024]{1,0:T(8,128)(2,1)S(1)}, bf16[256,1024]{1,0:T(8,128)(2,1)}, u32[]{:S(2)}) copy-start(bf16[256,1024]{1,0:T(8,128)(2,1)} %param.19) | copy-start | bytes 1572868
Sparse Core Ops, SparseCore 0:
  35.2 42.8 all-gather.1
where the time goes:
time: 155 us; the launch traced here: 153 us
  matrix products  70.4 us (45%)
  other arithmetic  20.7 us (13%)
  starting transfers between devices  18.8 us (12%)
  local copies, waits for them, and re-layouts  17.4 us (11%)
  between operations  13.8 us (9%)
  waiting for transfers between devices  11.7 us (8%)
    dot_general x24, matrix products, one_head(): jnp.einsum('dn,dm->nm', query_head, key_head, preferred_element_type=jnp....  32.3 us
    dot_general x24, matrix products, one_head(): jnp.einsum('nm,dm->dn', weights, value_head, preferred_element_type=jnp.f...  28.6 us
    reduce_sum x8, other arithmetic, one_head(): total = total + extra.sum(axis=1, keepdims=True)  11 us
    all_to_all x1, waiting for transfers between devices, per_device(): lax.all_to_all(packed.astype(jnp.bfloat16).reshape(lanes, capacity * CLUS...  10.4 us
    all_to_all x1, starting transfers between devices, per_device(): lax.all_to_all(sent_ids, 'ball', split_axis=0, concat_axis=0, tiled=True)  7.57 us
    all_to_all x1, starting transfers between devices, per_device(): lax.all_to_all(packed.astype(jnp.bfloat16).reshape(lanes, capacity * CLUS...  6.84 us
    reduce_sum x8, other arithmetic, one_head(): total = exponents[0].sum(axis=1, keepdims=True)  5.86 us
    all_to_all x1, starting transfers between devices, per_device(): lax.all_to_all(outgoing, 'ball', split_axis=0, concat_axis=0, tiled=True)  4.37 us
  transfers between devices with their start and end apart: 4, of which 2 were waited for; matrix products, arithmetic and copies ran while one was open for 65% of the time, Pallas kernels for 0%

commit v1 on v0

v1 whole, which is shorter than its diff:
```python
import functools
import math

import jax
import jax.numpy as jnp
from jax import lax
from jax.experimental import pallas as pl
from jax.experimental.pallas import tpu as pltpu
from jax.sharding import PartitionSpec as P

MESH = pl.DeviceIdType.MESH
BF = jnp.bfloat16
F32 = jnp.float32
HEADS = 8
HEAD = 32
C = 256
ROWS = 1024
CLUSTER = 64
CLUSTERS = 16
LANES = 16
POOL = 16
POOLED = ROWS // POOL
CHIPS = 8
QB = 512
QBLOCKS = ROWS // QB
ROW_CHUNK = 256
SCALE = math.log2(math.e) / math.sqrt(HEAD)


def norm_rows(x, gain):
    x = x.astype(F32)
    scale = lax.rsqrt(jnp.mean(x * x, axis=1, keepdims=True) + 1e-6)
    return (x * scale * gain).astype(BF)


def kernel(
    dest, x_ref, gain_a, wqk, wv, wout, gain_m, wup, wdown, out,
    normed, settled, qz, far_qz, keys, vals, pool, pvals, score, near_sum, near_max, near_t, far_t,
    send, recv, back_send, back_recv,
    out_sems, in_sems, bout_sems, bin_sems, pout_sems, pin_sems,
):
    me = lax.axis_index("ball")
    spot = lax.axis_index("region")
    chip, core = spot // 2, spot % 2

    def lane(offset):
        return {"ball": lax.rem(me + offset + LANES, LANES)}

    def chip_at(offset):
        return {"region": lax.rem(chip + offset + CHIPS, CHIPS) * 2 + core}

    partner = {"region": chip * 2 + 1 - core}

    barrier = pltpu.get_barrier_semaphore()
    for d in range(1, LANES):
        pl.semaphore_signal(barrier, inc=1, device_id=lane(d), device_id_type=MESH)
    for d in range(1, CHIPS):
        pl.semaphore_signal(barrier, inc=1, device_id=chip_at(d), device_id_type=MESH)
    pl.semaphore_signal(barrier, inc=1, device_id=partner, device_id_type=MESH)

    offsets = [lax.bitwise_and((dest[c] // CLUSTERS) - me + LANES, LANES - 1) for c in range(CLUSTERS)]
    first, second, active, upto = [], [], [], []
    count = jnp.int32(0)
    for d in range(LANES):
        lo, hi, hit = jnp.int32(CLUSTERS - 1), jnp.int32(0), jnp.int32(0)
        for c in range(CLUSTERS):
            same = offsets[c] == d
            lo = jnp.minimum(lo, jnp.where(same, c, CLUSTERS - 1))
            hi = jnp.maximum(hi, jnp.where(same, c, 0))
            hit = jnp.maximum(hit, jnp.where(same, 1, 0))
        count = count + hit
        first.append(lo)
        second.append(hi)
        active.append(hit)
        upto.append(count)

    def norm_chunk(i, _):
        n = norm_rows(x_ref[pl.ds(pl.multiple_of(i * ROW_CHUNK, ROW_CHUNK), ROW_CHUNK), :], gain_a[...])
        normed[pl.ds(i * (ROW_CHUNK // CLUSTER), ROW_CHUNK // CLUSTER)] = n.reshape(
            ROW_CHUNK // CLUSTER, CLUSTER, C
        )
        return 0

    lax.fori_loop(0, ROWS // ROW_CHUNK, norm_chunk, 0)
    for d in range(LANES):
        held = recv if d == 0 else send
        held[2 * d] = normed[first[d]]
        held[2 * d + 1] = normed[second[d]]

    pl.semaphore_wait(barrier, LANES - 1 + CHIPS - 1 + 1)
    sends = []
    for d in range(1, LANES):
        copy = pltpu.make_async_remote_copy(
            src_ref=send.at[pl.ds(2 * d, 2)], dst_ref=recv.at[pl.ds(2 * d, 2)],
            send_sem=out_sems.at[d], recv_sem=in_sems.at[d], device_id=lane(d), device_id_type=MESH,
        )
        copy.start()
        sends.append(copy)

    def project(source, qz):
        states = source[...].reshape(ROWS, C)
        turned = states.T
        query_t = jnp.dot(wqk[:, :C].T, turned, preferred_element_type=F32).astype(BF)
        for h in range(HEADS):
            at = h % 4 * HEAD
            qz[h, at:at + HEAD, :] = query_t[h * HEAD:(h + 1) * HEAD, :]
        keys[...] = jnp.dot(states, wqk[:, C:], preferred_element_type=F32).astype(BF)
        value_t = jnp.dot(wv[...].T, turned, preferred_element_type=F32).astype(BF)
        for h in range(HEADS):
            vals[h, :HEAD, :] = value_t[h * HEAD:(h + 1) * HEAD, :]

    qz[...] = jnp.zeros_like(qz)
    far_qz[...] = jnp.zeros_like(far_qz)
    for h in range(HEADS):
        vals[h, HEAD:, :] = jnp.ones((16, ROWS), BF)
        pvals[h, HEAD:, :] = jnp.ones((16, ROWS), BF)
    project(normed, qz)

    row = lax.broadcasted_iota(jnp.int32, (POOLED, ROWS), 0)
    col = lax.broadcasted_iota(jnp.int32, (POOLED, ROWS), 1)
    pooling = jnp.where(col // POOL == row, 1.0 / math.sqrt(POOL), 0.0).astype(BF)
    pool[:POOLED, :C] = jnp.dot(pooling, keys[...], preferred_element_type=F32).astype(BF)
    value_rows = jnp.dot(normed[...].reshape(ROWS, C), wv[...], preferred_element_type=F32).astype(BF)
    pool[:POOLED, C:] = jnp.dot(pooling, value_rows, preferred_element_type=F32).astype(BF)
    pooled_sends = []
    for d in range(1, CHIPS):
        copy = pltpu.make_async_remote_copy(
            src_ref=pool.at[pl.ds(0, POOLED)], dst_ref=pool.at[pl.ds(d * POOLED, POOLED)],
            send_sem=pout_sems.at[d], recv_sem=pin_sems.at[d], device_id=chip_at(d), device_id_type=MESH,
        )
        copy.start()
        pooled_sends.append(copy)

    def attend(qz, key_ref, value_ref, finish):
        def block(i, _):
            h, b = i // QBLOCKS, i % QBLOCKS
            cols = pl.ds(pl.multiple_of(b * QB, QB), QB)
            top = jnp.full((8, QB), -jnp.inf, F32)
            for c in range(ROWS // ROW_CHUNK):
                rows = pl.ds(c * ROW_CHUNK, ROW_CHUNK)
                k = key_ref[rows, pl.ds(pl.multiple_of(h // 4 * 128, 128), 128)]
                s = jnp.dot(k, qz[h, :, cols], preferred_element_type=F32)
                score[rows, :] = s
                for j in range(ROW_CHUNK // 8):
                    top = jnp.maximum(top, s[j * 8:(j + 1) * 8])
            top = jnp.max(top, axis=0, keepdims=True)
            total = jnp.zeros((48, QB), F32)
            for c in range(ROWS // ROW_CHUNK):
                rows = pl.ds(c * ROW_CHUNK, ROW_CHUNK)
                p = jnp.exp2((score[rows, :] - top) * SCALE).astype(BF)
                total = total + jnp.dot(value_ref[h, :, rows], p, preferred_element_type=F32)
            finish(h, cols, top, total)
            return 0

        lax.fori_loop(0, HEADS * QBLOCKS, block, 0)

    def keep(h, cols, top, total):
        near_sum[h, :, cols] = total
        near_max[h, :, cols] = jnp.broadcast_to(top, (8, QB))

    def head_rows(h):
        return pl.ds(pl.multiple_of(h * HEAD, HEAD), HEAD)

    def close(total):
        return (total[:HEAD] / total[HEAD:HEAD + 1]).astype(BF)

    def merge(h, cols, top, total):
        before = near_max[h, :1, cols]
        both = jnp.maximum(before, top)
        whole = near_sum[h, :, cols] * jnp.exp2((before - both) * SCALE) + total * jnp.exp2((top - both) * SCALE)
        near_t[head_rows(h), cols] = close(whole)

    def far_done(h, cols, top, total):
        far_t[head_rows(h), cols] = close(total)

    attend(qz, keys, vals, keep)

    for copy in pooled_sends:
        copy.wait()
    across = pltpu.make_async_remote_copy(
        src_ref=pool.at[pl.ds(0, ROWS // 2)], dst_ref=pool.at[pl.ds(ROWS // 2, ROWS // 2)],
        send_sem=pout_sems.at[0], recv_sem=pin_sems.at[0], device_id=partner, device_id_type=MESH,
    )
    across.start()

    for copy in sends:
        copy.wait()
    for j in range(LANES // 2):
        d = jnp.int32(0)
        for k in range(LANES):
            d = d + jnp.where(upto[k] <= j, 1, 0)
        d = jnp.minimum(d, LANES - 1)
        settled[2 * j] = recv[2 * d]
        settled[2 * j + 1] = recv[2 * d + 1]
    project(settled, far_qz)
    attend(far_qz, keys, vals, far_done)
    settled[...] = far_t[...].T.reshape(CLUSTERS, CLUSTER, C)
    for d in range(LANES):
        held = back_recv if d == 0 else back_send
        j = jnp.minimum(upto[d] - active[d], LANES // 2 - 1)
        held[2 * d] = settled[2 * j]
        held[2 * d + 1] = settled[2 * j + 1]
    backs = []
    for d in range(1, LANES):
        copy = pltpu.make_async_remote_copy(
            src_ref=back_send.at[pl.ds(2 * d, 2)], dst_ref=back_recv.at[pl.ds(2 * d, 2)],
            send_sem=bout_sems.at[d], recv_sem=bin_sems.at[d], device_id=lane(-d), device_id_type=MESH,
        )
        copy.start()
        backs.append(copy)

    across.wait()
    turned = pool[:, C:].T
    for h in range(HEADS):
        pvals[h, :HEAD, :] = turned[h * HEAD:(h + 1) * HEAD, :]
    attend(qz, pool, pvals, merge)

    for copy in backs:
        copy.wait()
    for c in range(CLUSTERS):
        rank = jnp.int32(0)
        for e in range(c):
            rank = rank + jnp.where(offsets[e] == offsets[c], 1, 0)
        settled[c] = back_recv[2 * offsets[c] + jnp.minimum(rank, 1)]

    def tail(i, _):
        rows = pl.ds(pl.multiple_of(i * ROW_CHUNK, ROW_CHUNK), ROW_CHUNK)
        near = near_t[:, rows].T
        far = settled[pl.ds(i * (ROW_CHUNK // CLUSTER), ROW_CHUNK // CLUSTER)].reshape(ROW_CHUNK, C)
        after = (
            x_ref[rows, :].astype(F32)
            + jnp.dot(near, wout[...], preferred_element_type=F32)
            + jnp.dot(far, wout[...], preferred_element_type=F32)
        ).astype(BF)
        mlp_in = norm_rows(after, gain_m[...])
        hidden = jax.nn.gelu(jnp.dot(mlp_in, wup[...], preferred_element_type=F32), approximate=True).astype(BF)
        out[rows, :] = (
            after.astype(F32) + jnp.dot(hidden, wdown[...], preferred_element_type=F32)
        ).astype(BF)
        return 0

    lax.fori_loop(0, ROWS // ROW_CHUNK, tail, 0)


def per_device(points, gain_attn, w_query_key, w_value, w_out, gain_mlp, w_up, w_down, cluster_dest):
    vmem = pl.BlockSpec(memory_space=pltpu.VMEM)
    clusters = pltpu.VMEM((CLUSTERS, CLUSTER, C), BF)
    slots = pltpu.VMEM((2 * LANES, CLUSTER, C), BF)
    values = pltpu.VMEM((HEADS, 48, ROWS), BF)
    turned = pltpu.VMEM((C, ROWS), BF)
    result = pl.pallas_call(
        kernel,
        out_shape=jax.ShapeDtypeStruct((ROWS, C), BF),
        in_specs=[pl.BlockSpec(memory_space=pltpu.SMEM)] + [vmem] * 8,
        out_specs=vmem,
        scratch_shapes=[
            clusters, clusters,
            pltpu.VMEM((HEADS, 128, ROWS), BF),
            pltpu.VMEM((HEADS, 128, ROWS), BF),
            pltpu.VMEM((ROWS, C), BF),
            values,
            pltpu.VMEM((ROWS, 2 * C), BF),
            values,
            pltpu.VMEM((ROWS, QB), F32),
            pltpu.VMEM((HEADS, 48, ROWS), F32),
            pltpu.VMEM((HEADS, 8, ROWS), F32),
            turned, turned,
            slots, slots, slots, slots,
        ]
        + [pltpu.SemaphoreType.DMA((LANES,))] * 4
        + [pltpu.SemaphoreType.DMA((CHIPS,))] * 2,
        compiler_params=pltpu.CompilerParams(
            collective_id=0, has_side_effects=True, vmem_limit_bytes=60 * 1024 * 1024
        ),
        name="block",
    )(
        cluster_dest.reshape(CLUSTERS), points.reshape(ROWS, C), gain_attn.reshape(1, C), w_query_key,
        w_value, w_out, gain_mlp.reshape(1, C), w_up, w_down,
    )
    return result.reshape(points.shape)


def solution(mesh):
    placed = (P("ball", "region", None, None),) + (P(),) * 7 + (P("ball", "region", None),)
    return jax.shard_map(
        per_device, mesh=mesh, in_specs=placed, out_specs=P("ball", "region", None, None), check_vma=False
    )
```

time: 155 us -> 65.4 us (0.42); the launches traced: 153 us -> 65.3 us
  matrix products: 70.4 us -> 0 us
  Pallas kernels: 0 us -> 63.4 us
  other arithmetic: 20.7 us -> 0 us
  starting transfers between devices: 18.8 us -> 0 us
  local copies, waits for them, and re-layouts: 17.4 us -> 1.87 us
  between operations: 13.8 us -> 0.01 us
  waiting for transfers between devices: 11.7 us -> 0 us
    dot_general x59 -> x0, matrix products: 70.4 us -> none  [the longest x24 32.3 us: one_head(): jnp.einsum('dn,dm->nm', query_head, key_head, preferred_element_type=jnp....]
    pallas_call x0 -> x1, Pallas kernels: none -> 63.4 us  [per_device(): pl.pallas_call(kernel, out_shape=jax.ShapeDtypeStruct((ROWS, C), BF), in_...]
    all_to_all x3 -> x0, starting transfers between devices: 18.8 us -> none  [the longest x1 7.57 us: per_device(): lax.all_to_all(sent_ids, 'ball', split_axis=0, concat_axis=0, tiled=True)]
    reduce_sum x19 -> x0, other arithmetic: 17.3 us -> none  [the longest x8 11 us: one_head(): total = total + extra.sum(axis=1, keepdims=True)]
    all_to_all x3 -> x0, waiting for transfers between devices: 10.4 us -> none  [the longest x1 10.4 us: per_device(): lax.all_to_all(packed.astype(jnp.bfloat16).reshape(lanes, capacity * CLUS...]
    reshape x7 -> x0, local copies, waits for them, and re-layouts: 7.23 us -> none  [the longest x1 2.35 us: per_device(): packed.astype(jnp.bfloat16).reshape(lanes, capacity * CLUSTER, inner)]
    convert_element_type x4 -> x0, local copies, waits for them, and re-layouts: 2.76 us -> none  [the longest x2 1.43 us: per_device(): flat.astype(jnp.float32) + near_out]
    unnamed x26 -> x1, local copies, waits for them, and re-layouts: 3.94 us -> 1.87 us
  transfers between devices with their start and end apart: 4 -> 0, of which waited for: 2 -> 0; matrix products, arithmetic and copies ran while one was open for 65% -> 0% of each run, Pallas kernels for 0% -> 0%
where the time goes in v1:
time: 65.4 us; the launch traced here: 65.3 us
  Pallas kernels  63.4 us (97%)
  local copies, waits for them, and re-layouts  1.87 us (3%)
    pallas_call x1, Pallas kernels, per_device(): pl.pallas_call(kernel, out_shape=jax.ShapeDtypeStruct((ROWS, C), BF), in_...  63.4 us
    unnamed x1, local copies, waits for them, and re-layouts  1.87 us

profile of v1, /device:TPU:1, one launch (start us, length us, event | category | flops | bytes accessed | tf_op | source)
XLA Modules:
  0.0 65.3 jit_solution(13193491255740021495)
XLA Ops:
  0.0 63.4 %block.1 = bf16[1024,256]{1,0:T(8,128)(2,1)} custom-call(s32[16]{0:T(128)} %bitcast.9, bf16[1024,256]{1,0:T(8,128)(2,1)} %bitcast.6, f32[1,256]{1,0:T(1,128)} %bitcast.7, bf16[256,512]{1,0:T(8,128)(2,1)} %wqk.1, bf16[256,256]{1,0:T(8,128)(2,1)} %wv.1, bf16[256,256]{1,0:T(8,128)(2,1)} %wout.1, f32[1,256]{1,0:T(1,128)} %bitcast.8, bf16[256,1024]{1,0:T(8,128)(2,1)} %wup.1, ...), custom_call_target="tpu_custom_call" | custom-call | tf_op jit(solution)/shard_map/block/pallas_call | solution.py:251
  63.4 1.9 %copy.11 = bf16[1,1,1024,256]{3,2,1,0:T(8,128)(2,1)} copy(bf16[1,1,1024,256]{3,2,1,0:T(8,128)(2,1)} %bitcast.5) | data formatting | bytes 1048576

commit v2 on v1

--- a/solution.py
+++ b/solution.py
@@ -23,6 +23,10 @@
 CHIPS = 8
 QB = 512
 QBLOCKS = ROWS // QB
+BLOCKS = HEADS * QBLOCKS
+GROUP = 2
+PIECE = 128
+DEPTH = 256
 ROW_CHUNK = 256
 SCALE = math.log2(math.e) / math.sqrt(HEAD)
 
@@ -35,7 +39,7 @@
 
 def kernel(
     dest, x_ref, gain_a, wqk, wv, wout, gain_m, wup, wdown, out,
-    normed, settled, qz, far_qz, keys, vals, pool, pvals, score, near_sum, near_max, near_t, far_t,
+    normed, settled, near_q, far_q, keys, vals, pool, score, weight, tops, near_sum, near_max, near_t, far_t,
     send, recv, back_send, back_recv,
     out_sems, in_sems, bout_sems, bin_sems, pout_sems, pin_sems,
 ):
@@ -58,18 +62,17 @@
         pl.semaphore_signal(barrier, inc=1, device_id=chip_at(d), device_id_type=MESH)
     pl.semaphore_signal(barrier, inc=1, device_id=partner, device_id_type=MESH)
 
-    offsets = [lax.bitwise_and((dest[c] // CLUSTERS) - me + LANES, LANES - 1) for c in range(CLUSTERS)]
+    offsets = [lax.bitwise_and(lax.shift_right_arithmetic(dest[c], 4) - me, LANES - 1) for c in range(CLUSTERS)]
     first, second, active, upto = [], [], [], []
     count = jnp.int32(0)
     for d in range(LANES):
-        lo, hi, hit = jnp.int32(CLUSTERS - 1), jnp.int32(0), jnp.int32(0)
+        lo, hi = jnp.int32(CLUSTERS), jnp.int32(0)
         for c in range(CLUSTERS):
-            same = offsets[c] == d
-            lo = jnp.minimum(lo, jnp.where(same, c, CLUSTERS - 1))
-            hi = jnp.maximum(hi, jnp.where(same, c, 0))
-            hit = jnp.maximum(hit, jnp.where(same, 1, 0))
+            hi = jnp.where(offsets[c] == d, c, hi)
+            lo = jnp.where(offsets[CLUSTERS - 1 - c] == d, CLUSTERS - 1 - c, lo)
+        hit = jnp.where(lo < CLUSTERS, 1, 0)
         count = count + hit
-        first.append(lo)
+        first.append(jnp.minimum(lo, CLUSTERS - 1))
         second.append(hi)
         active.append(hit)
         upto.append(count)
@@ -97,29 +100,31 @@
         copy.start()
         sends.append(copy)
 
-    def project(source, qz):
+    def set_keys(rows):
+        for h in range(HEADS):
+            keys[h] = rows[:, h * HEAD:(h + 1) * HEAD]
+
+    def set_values(value_t):
+        for h in range(HEADS):
+            vals[h, :HEAD, :] = value_t[h * HEAD:(h + 1) * HEAD, :]
+
+    def project(source, query_t):
         states = source[...].reshape(ROWS, C)
         turned = states.T
-        query_t = jnp.dot(wqk[:, :C].T, turned, preferred_element_type=F32).astype(BF)
-        for h in range(HEADS):
-            at = h % 4 * HEAD
-            qz[h, at:at + HEAD, :] = query_t[h * HEAD:(h + 1) * HEAD, :]
-        keys[...] = jnp.dot(states, wqk[:, C:], preferred_element_type=F32).astype(BF)
-        value_t = jnp.dot(wv[...].T, turned, preferred_element_type=F32).astype(BF)
-        for h in range(HEADS):
-            vals[h, :HEAD, :] = value_t[h * HEAD:(h + 1) * HEAD, :]
-
-    qz[...] = jnp.zeros_like(qz)
-    far_qz[...] = jnp.zeros_like(far_qz)
+        query_t[...] = jnp.dot(wqk[:, :C].T, turned, preferred_element_type=F32).astype(BF)
+        key_rows = jnp.dot(states, wqk[:, C:], preferred_element_type=F32).astype(BF)
+        set_keys(key_rows)
+        set_values(jnp.dot(wv[...].T, turned, preferred_element_type=F32).astype(BF))
+        return key_rows
+
     for h in range(HEADS):
         vals[h, HEAD:, :] = jnp.ones((16, ROWS), BF)
-        pvals[h, HEAD:, :] = jnp.ones((16, ROWS), BF)
-    project(normed, qz)
+    key_rows = project(normed, near_q)
 
     row = lax.broadcasted_iota(jnp.int32, (POOLED, ROWS), 0)
     col = lax.broadcasted_iota(jnp.int32, (POOLED, ROWS), 1)
     pooling = jnp.where(col // POOL == row, 1.0 / math.sqrt(POOL), 0.0).astype(BF)
-    pool[:POOLED, :C] = jnp.dot(pooling, keys[...], preferred_element_type=F32).astype(BF)
+    pool[:POOLED, :C] = jnp.dot(pooling, key_rows, preferred_element_type=F32).astype(BF)
     value_rows = jnp.dot(normed[...].reshape(ROWS, C), wv[...], preferred_element_type=F32).astype(BF)
     pool[:POOLED, C:] = jnp.dot(pooling, value_rows, preferred_element_type=F32).astype(BF)
     pooled_sends = []
@@ -131,28 +136,76 @@
         copy.start()
         pooled_sends.append(copy)
 
-    def attend(qz, key_ref, value_ref, finish):
-        def block(i, _):
-            h, b = i // QBLOCKS, i % QBLOCKS
-            cols = pl.ds(pl.multiple_of(b * QB, QB), QB)
-            top = jnp.full((8, QB), -jnp.inf, F32)
-            for c in range(ROWS // ROW_CHUNK):
-                rows = pl.ds(c * ROW_CHUNK, ROW_CHUNK)
-                k = key_ref[rows, pl.ds(pl.multiple_of(h // 4 * 128, 128), 128)]
-                s = jnp.dot(k, qz[h, :, cols], preferred_element_type=F32)
-                score[rows, :] = s
-                for j in range(ROW_CHUNK // 8):
-                    top = jnp.maximum(top, s[j * 8:(j + 1) * 8])
-            top = jnp.max(top, axis=0, keepdims=True)
-            total = jnp.zeros((48, QB), F32)
-            for c in range(ROWS // ROW_CHUNK):
-                rows = pl.ds(c * ROW_CHUNK, ROW_CHUNK)
-                p = jnp.exp2((score[rows, :] - top) * SCALE).astype(BF)
-                total = total + jnp.dot(value_ref[h, :, rows], p, preferred_element_type=F32)
-            finish(h, cols, top, total)
+    def attend(query_t, finish):
+        def spot_of(i):
+            return i // QBLOCKS, pl.ds(pl.multiple_of(i % QBLOCKS * QB, QB), QB)
+
+        def head_rows(h):
+            return pl.ds(pl.multiple_of(h * HEAD, HEAD), HEAD)
+
+        def scores_of(i, slot, r, top):
+            h, cols = spot_of(i)
+            rows = pl.ds(r * PIECE, PIECE)
+            s = jnp.dot(keys[h, rows, :], query_t[head_rows(h), cols], preferred_element_type=F32)
+            score[slot, rows, :] = s
+            for j in range(PIECE // 8):
+                top = jnp.maximum(top, s[j * 8:(j + 1) * 8])
+            return top
+
+        def sum_of(h, slot, c, total):
+            rows = pl.ds(c * DEPTH, DEPTH)
+            return total + jnp.dot(vals[h, :, rows], weight[slot, rows, :], preferred_element_type=F32)
+
+        def top_of(slot):
+            return jnp.max(tops[slot], axis=0, keepdims=True)
+
+        low = jnp.full((8, QB), -jnp.inf, F32)
+        none = jnp.zeros((48, QB), F32)
+
+        def step(g, even):
+            for b in range(GROUP):
+                i = g * GROUP + b
+                now = b if even else GROUP + b
+                other = GROUP + b if even else b
+                old = jnp.maximum(i - GROUP, 0)
+                new = jnp.minimum(i + GROUP, BLOCKS - 1)
+                old_head, old_cols = spot_of(old)
+                old_top = top_of(other)
+                top = top_of(now)
+                new_top, total = low, none
+                for r in range(ROWS // PIECE):
+                    rows = pl.ds(r * PIECE, PIECE)
+                    new_top = scores_of(new, other, r, new_top)
+                    weight[now, rows, :] = jnp.exp2((score[now, rows, :] - top) * SCALE).astype(BF)
+                    if (r + 1) * PIECE % DEPTH == 0:
+                        total = sum_of(old_head, other, (r + 1) * PIECE // DEPTH - 1, total)
+                tops[other] = new_top
+                finish(old_head, old_cols, old_top, total)
+
+        for b in range(GROUP):
+            top = low
+            for r in range(ROWS // PIECE):
+                top = scores_of(b, b, r, top)
+            tops[b] = top
+
+        def pair(t, _):
+            @pl.when(2 * t < BLOCKS // GROUP)
+            def _():
+                step(2 * t, True)
+
+            @pl.when(2 * t + 1 < BLOCKS // GROUP)
+            def _():
+                step(2 * t + 1, False)
+
             return 0
 
-        lax.fori_loop(0, HEADS * QBLOCKS, block, 0)
+        lax.fori_loop(0, BLOCKS // GROUP // 2, pair, 0)
+        for b in range(GROUP):
+            h, cols = spot_of(BLOCKS - GROUP + b)
+            total = none
+            for c in range(ROWS // DEPTH):
+                total = sum_of(h, GROUP + b, c, total)
+            finish(h, cols, top_of(GROUP + b), total)
 
     def keep(h, cols, top, total):
         near_sum[h, :, cols] = total
@@ -173,7 +226,7 @@
     def far_done(h, cols, top, total):
         far_t[head_rows(h), cols] = close(total)
 
-    attend(qz, keys, vals, keep)
+    attend(near_q, keep)
 
     for copy in pooled_sends:
         copy.wait()
@@ -192,8 +245,8 @@
         d = jnp.minimum(d, LANES - 1)
         settled[2 * j] = recv[2 * d]
         settled[2 * j + 1] = recv[2 * d + 1]
-    project(settled, far_qz)
-    attend(far_qz, keys, vals, far_done)
+    project(settled, far_q)
+    attend(far_q, far_done)
     settled[...] = far_t[...].T.reshape(CLUSTERS, CLUSTER, C)
     for d in range(LANES):
         held = back_recv if d == 0 else back_send
@@ -210,10 +263,9 @@
         backs.append(copy)
 
     across.wait()
-    turned = pool[:, C:].T
-    for h in range(HEADS):
-        pvals[h, :HEAD, :] = turned[h * HEAD:(h + 1) * HEAD, :]
-    attend(qz, pool, pvals, merge)
+    set_keys(pool[:, :C])
+    set_values(pool[:, C:].T)
+    attend(near_q, merge)
 
     for copy in backs:
         copy.wait()
@@ -246,7 +298,6 @@
     vmem = pl.BlockSpec(memory_space=pltpu.VMEM)
     clusters = pltpu.VMEM((CLUSTERS, CLUSTER, C), BF)
     slots = pltpu.VMEM((2 * LANES, CLUSTER, C), BF)
-    values = pltpu.VMEM((HEADS, 48, ROWS), BF)
     turned = pltpu.VMEM((C, ROWS), BF)
     result = pl.pallas_call(
         kernel,
@@ -255,13 +306,13 @@
         out_specs=vmem,
         scratch_shapes=[
             clusters, clusters,
-            pltpu.VMEM((HEADS, 128, ROWS), BF),
-            pltpu.VMEM((HEADS, 128, ROWS), BF),
-            pltpu.VMEM((ROWS, C), BF),
-            values,
+            turned, turned,
+            pltpu.VMEM((HEADS, ROWS, HEAD), BF),
+            pltpu.VMEM((HEADS, 48, ROWS), BF),
             pltpu.VMEM((ROWS, 2 * C), BF),
-            values,
-            pltpu.VMEM((ROWS, QB), F32),
+            pltpu.VMEM((2 * GROUP, ROWS, QB), F32),
+            pltpu.VMEM((2 * GROUP, ROWS, QB), BF),
+            pltpu.VMEM((2 * GROUP, 8, QB), F32),
             pltpu.VMEM((HEADS, 48, ROWS), F32),
             pltpu.VMEM((HEADS, 8, ROWS), F32),
             turned, turned,

time: 65.4 us -> 57.9 us (0.89)
  Pallas kernels: 63.4 us -> 55.9 us
    pallas_call x1, Pallas kernels: 63.4 us -> 55.9 us  [per_device(): pl.pallas_call(kernel, out_shape=jax.ShapeDtypeStruct((ROWS, C), BF), in_...]
where the time goes in v2:
time: 57.9 us; the launch traced here: 57.8 us
  Pallas kernels  55.9 us (97%)
  local copies, waits for them, and re-layouts  1.87 us (3%)
    pallas_call x1, Pallas kernels, per_device(): pl.pallas_call(kernel, out_shape=jax.ShapeDtypeStruct((ROWS, C), BF), in_...  55.9 us
    unnamed x1, local copies, waits for them, and re-layouts  1.87 us

profile of v2, /device:TPU:1, one launch (start us, length us, event | category | flops | bytes accessed | tf_op | source)
XLA Modules:
  0.0 57.8 jit_solution(16763911273056699122)
XLA Ops:
  0.0 55.9 %block.1 = bf16[1024,256]{1,0:T(8,128)(2,1)} custom-call(s32[16]{0:T(128)} %bitcast.9, bf16[1024,256]{1,0:T(8,128)(2,1)} %bitcast.6, f32[1,256]{1,0:T(1,128)} %bitcast.7, bf16[256,512]{1,0:T(8,128)(2,1)} %wqk.1, bf16[256,256]{1,0:T(8,128)(2,1)} %wv.1, bf16[256,256]{1,0:T(8,128)(2,1)} %wout.1, f32[1,256]{1,0:T(1,128)} %bitcast.8, bf16[256,1024]{1,0:T(8,128)(2,1)} %wup.1, ...), custom_call_target="tpu_custom_call" | custom-call | tf_op jit(solution)/shard_map/block/pallas_call | solution.py:302
  55.9 1.9 %copy.11 = bf16[1,1,1024,256]{3,2,1,0:T(8,128)(2,1)} copy(bf16[1,1,1024,256]{3,2,1,0:T(8,128)(2,1)} %bitcast.5) | data formatting | bytes 1048576

commit v3 on v2

--- a/solution.py
+++ b/solution.py
@@ -27,6 +27,8 @@
 GROUP = 2
 PIECE = 128
 DEPTH = 256
+PARTS = 4
+PART = C // PARTS
 ROW_CHUNK = 256
 SCALE = math.log2(math.e) / math.sqrt(HEAD)
 
@@ -38,10 +40,11 @@
 
 
 def kernel(
-    dest, x_ref, gain_a, wqk, wv, wout, gain_m, wup, wdown, out,
+    dest, gain_a, gain_m, x_in, wqk_in, wv_in, wout_in, wup_in, wdown_in, out,
+    x_ref, wqk, wv, wout, wup, wdown,
     normed, settled, near_q, far_q, keys, vals, pool, score, weight, tops, near_sum, near_max, near_t, far_t,
     send, recv, back_send, back_recv,
-    out_sems, in_sems, bout_sems, bin_sems, pout_sems, pin_sems,
+    out_sems, in_sems, bout_sems, bin_sems, pout_sems, pin_sems, load_sems,
 ):
     me = lax.axis_index("ball")
     spot = lax.axis_index("region")
@@ -55,6 +58,14 @@
 
     partner = {"region": chip * 2 + 1 - core}
 
+    loads = [
+        pltpu.make_async_copy(source, held, load_sems.at[k])
+        for k, (source, held) in enumerate(
+            ((x_in, x_ref), (wqk_in, wqk), (wv_in, wv), (wout_in, wout), (wup_in, wup), (wdown_in, wdown))
+        )
+    ]
+    for load in loads:
+        load.start()
     barrier = pltpu.get_barrier_semaphore()
     for d in range(1, LANES):
         pl.semaphore_signal(barrier, inc=1, device_id=lane(d), device_id_type=MESH)
@@ -77,6 +88,8 @@
         active.append(hit)
         upto.append(count)
 
+    loads[0].wait()
+
     def norm_chunk(i, _):
         n = norm_rows(x_ref[pl.ds(pl.multiple_of(i * ROW_CHUNK, ROW_CHUNK), ROW_CHUNK), :], gain_a[...])
         normed[pl.ds(i * (ROW_CHUNK // CLUSTER), ROW_CHUNK // CLUSTER)] = n.reshape(
@@ -119,6 +132,8 @@
 
     for h in range(HEADS):
         vals[h, HEAD:, :] = jnp.ones((16, ROWS), BF)
+    for load in loads[1:3]:
+        load.wait()
     key_rows = project(normed, near_q)
 
     row = lax.broadcasted_iota(jnp.int32, (POOLED, ROWS), 0)
@@ -136,7 +151,7 @@
         copy.start()
         pooled_sends.append(copy)
 
-    def attend(query_t, finish):
+    def attend(query_t, finish, between=None):
         def spot_of(i):
             return i // QBLOCKS, pl.ds(pl.multiple_of(i % QBLOCKS * QB, QB), QB)
 
@@ -162,7 +177,7 @@
         low = jnp.full((8, QB), -jnp.inf, F32)
         none = jnp.zeros((48, QB), F32)
 
-        def step(g, even):
+        def step(g, even, last=False):
             for b in range(GROUP):
                 i = g * GROUP + b
                 now = b if even else GROUP + b
@@ -170,17 +185,25 @@
                 old = jnp.maximum(i - GROUP, 0)
                 new = jnp.minimum(i + GROUP, BLOCKS - 1)
                 old_head, old_cols = spot_of(old)
+                head, cols = spot_of(i)
                 old_top = top_of(other)
                 top = top_of(now)
-                new_top, total = low, none
+                new_top, total, last_total = low, none, none
                 for r in range(ROWS // PIECE):
                     rows = pl.ds(r * PIECE, PIECE)
-                    new_top = scores_of(new, other, r, new_top)
+                    if not last:
+                        new_top = scores_of(new, other, r, new_top)
                     weight[now, rows, :] = jnp.exp2((score[now, rows, :] - top) * SCALE).astype(BF)
                     if (r + 1) * PIECE % DEPTH == 0:
-                        total = sum_of(old_head, other, (r + 1) * PIECE // DEPTH - 1, total)
-                tops[other] = new_top
+                        part = (r + 1) * PIECE // DEPTH - 1
+                        total = sum_of(old_head, other, part, total)
+                        if last:
+                            last_total = sum_of(head, now, part, last_total)
                 finish(old_head, old_cols, old_top, total)
+                if last:
+                    finish(head, cols, top, last_total)
+                else:
+                    tops[other] = new_top
 
         for b in range(GROUP):
             top = low
@@ -188,24 +211,29 @@
                 top = scores_of(b, b, r, top)
             tops[b] = top
 
+        pairs = BLOCKS // GROUP // 2
+
         def pair(t, _):
-            @pl.when(2 * t < BLOCKS // GROUP)
+            @pl.when(t < pairs)
             def _():
                 step(2 * t, True)
 
-            @pl.when(2 * t + 1 < BLOCKS // GROUP)
+            if between is not None:
+                @pl.when(t >= 1)
+                def _():
+                    between(t - 1)
+
+            @pl.when(t < pairs - 1)
             def _():
                 step(2 * t + 1, False)
 
+            @pl.when(t == pairs - 1)
+            def _():
+                step(2 * t + 1, False, last=True)
+
             return 0
 
-        lax.fori_loop(0, BLOCKS // GROUP // 2, pair, 0)
-        for b in range(GROUP):
-            h, cols = spot_of(BLOCKS - GROUP + b)
-            total = none
-            for c in range(ROWS // DEPTH):
-                total = sum_of(h, GROUP + b, c, total)
-            finish(h, cols, top_of(GROUP + b), total)
+        lax.fori_loop(0, pairs, pair, 0)
 
     def keep(h, cols, top, total):
         near_sum[h, :, cols] = total
@@ -224,7 +252,11 @@
         near_t[head_rows(h), cols] = close(whole)
 
     def far_done(h, cols, top, total):
-        far_t[head_rows(h), cols] = close(total)
+        rows = pl.ds(pl.multiple_of(h % 2 * HEAD, HEAD), HEAD)
+        block = close(total)
+        for k in range(QB // (2 * CLUSTER)):
+            at = h // 2 * (LANES // 2) + cols.start // (2 * CLUSTER) + k
+            far_t[at, rows, :] = block[:, k * 2 * CLUSTER:(k + 1) * 2 * CLUSTER]
 
     attend(near_q, keep)
 
@@ -238,42 +270,55 @@
 
     for copy in sends:
         copy.wait()
+    picks = []
     for j in range(LANES // 2):
         d = jnp.int32(0)
         for k in range(LANES):
             d = d + jnp.where(upto[k] <= j, 1, 0)
         d = jnp.minimum(d, LANES - 1)
+        picks.append(d)
         settled[2 * j] = recv[2 * d]
         settled[2 * j + 1] = recv[2 * d + 1]
     project(settled, far_q)
-    attend(far_q, far_done)
-    settled[...] = far_t[...].T.reshape(CLUSTERS, CLUSTER, C)
-    for d in range(LANES):
-        held = back_recv if d == 0 else back_send
-        j = jnp.minimum(upto[d] - active[d], LANES // 2 - 1)
-        held[2 * d] = settled[2 * j]
-        held[2 * d + 1] = settled[2 * j + 1]
-    backs = []
-    for d in range(1, LANES):
-        copy = pltpu.make_async_remote_copy(
-            src_ref=back_send.at[pl.ds(2 * d, 2)], dst_ref=back_recv.at[pl.ds(2 * d, 2)],
-            send_sem=bout_sems.at[d], recv_sem=bin_sems.at[d], device_id=lane(-d), device_id_type=MESH,
-        )
-        copy.start()
-        backs.append(copy)
+    def back_copy(part, d):
+        at = part * LANES + d
+        return pltpu.make_async_remote_copy(
+            src_ref=back_send.at[at], dst_ref=back_recv.at[at],
+            send_sem=bout_sems.at[at], recv_sem=bin_sems.at[at], device_id=lane(-d), device_id_type=MESH,
+        )
+
+    def send_back(part):
+        for d in range(LANES):
+            held = back_recv if d == 0 else back_send
+            j = jnp.minimum(upto[d] - active[d], LANES // 2 - 1)
+            held[part * LANES + d] = far_t[part * (LANES // 2) + j]
+        for d in range(1, LANES):
+            back_copy(part, d).start()
+
+    attend(far_q, far_done, send_back)
+    send_back(PARTS - 1)
 
     across.wait()
     set_keys(pool[:, :C])
     set_values(pool[:, C:].T)
     attend(near_q, merge)
 
-    for copy in backs:
-        copy.wait()
+    for part in range(PARTS):
+        for d in range(1, LANES):
+            back_copy(part, d).wait()
+    for j in range(LANES // 2):
+        block = jnp.concatenate([back_recv[part * LANES + picks[j]] for part in range(PARTS)], axis=0)
+        normed[2 * j:2 * j + 2] = block.T.reshape(2, CLUSTER, C)
     for c in range(CLUSTERS):
+        at = jnp.int32(0)
+        for j in range(LANES // 2 - 1):
+            at = at + jnp.where(picks[j] < offsets[c], 2, 0)
         rank = jnp.int32(0)
         for e in range(c):
             rank = rank + jnp.where(offsets[e] == offsets[c], 1, 0)
-        settled[c] = back_recv[2 * offsets[c] + jnp.minimum(rank, 1)]
+        settled[c] = normed[at + jnp.minimum(rank, 1)]
+    for load in loads[3:]:
+        load.wait()
 
     def tail(i, _):
         rows = pl.ds(pl.multiple_of(i * ROW_CHUNK, ROW_CHUNK), ROW_CHUNK)
@@ -299,12 +344,16 @@
     clusters = pltpu.VMEM((CLUSTERS, CLUSTER, C), BF)
     slots = pltpu.VMEM((2 * LANES, CLUSTER, C), BF)
     turned = pltpu.VMEM((C, ROWS), BF)
+    parts = pltpu.VMEM((PARTS * LANES, PART, 2 * CLUSTER), BF)
+    anywhere = pl.BlockSpec(memory_space=pl.ANY)
+    moved = (points.reshape(ROWS, C), w_query_key, w_value, w_out, w_up, w_down)
     result = pl.pallas_call(
         kernel,
         out_shape=jax.ShapeDtypeStruct((ROWS, C), BF),
-        in_specs=[pl.BlockSpec(memory_space=pltpu.SMEM)] + [vmem] * 8,
+        in_specs=[pl.BlockSpec(memory_space=pltpu.SMEM)] + [vmem] * 2 + [anywhere] * 6,
         out_specs=vmem,
-        scratch_shapes=[
+        scratch_shapes=[pltpu.VMEM(a.shape, BF) for a in moved]
+        + [
             clusters, clusters,
             turned, turned,
             pltpu.VMEM((HEADS, ROWS, HEAD), BF),
@@ -315,18 +364,19 @@
             pltpu.VMEM((2 * GROUP, 8, QB), F32),
             pltpu.VMEM((HEADS, 48, ROWS), F32),
             pltpu.VMEM((HEADS, 8, ROWS), F32),
-            turned, turned,
-            slots, slots, slots, slots,
+            turned,
+            pltpu.VMEM((PARTS * LANES // 2, PART, 2 * CLUSTER), BF),
+            slots, slots, parts, parts,
         ]
-        + [pltpu.SemaphoreType.DMA((LANES,))] * 4
-        + [pltpu.SemaphoreType.DMA((CHIPS,))] * 2,
+        + [pltpu.SemaphoreType.DMA((LANES,))] * 2
+        + [pltpu.SemaphoreType.DMA((PARTS * LANES,))] * 2
+        + [pltpu.SemaphoreType.DMA((CHIPS,))] * 3,
         compiler_params=pltpu.CompilerParams(
             collective_id=0, has_side_effects=True, vmem_limit_bytes=60 * 1024 * 1024
         ),
         name="block",
     )(
-        cluster_dest.reshape(CLUSTERS), points.reshape(ROWS, C), gain_attn.reshape(1, C), w_query_key,
-        w_value, w_out, gain_mlp.reshape(1, C), w_up, w_down,
+        cluster_dest.reshape(CLUSTERS), gain_attn.reshape(1, C), gain_mlp.reshape(1, C), *moved
     )
     return result.reshape(points.shape)
 

time: 57.9 us -> 53.5 us (0.924)
  the two profiles are of different devices: /device:TPU:1 before, /device:TPU:8 now
where the time goes in v3:
time: 53.5 us; the launch traced here: 53.3 us
  Pallas kernels  51.4 us (96%)
  local copies, waits for them, and re-layouts  1.87 us (3%)
    pallas_call x1, Pallas kernels, per_device(): pl.pallas_call(kernel, out_shape=jax.ShapeDtypeStruct((ROWS, C), BF), in_...  51.4 us
    unnamed x1, local copies, waits for them, and re-layouts  1.87 us

profile of v3, /device:TPU:8, one launch (start us, length us, event | category | flops | bytes accessed | tf_op | source)
XLA Modules:
  0.0 53.3 jit_solution(1956865482299740659)
XLA Ops:
  0.0 51.4 %block.1 = bf16[1024,256]{1,0:T(8,128)(2,1)} custom-call(s32[16]{0:T(128)} %bitcast.9, f32[1,256]{1,0:T(1,128)} %bitcast.7, f32[1,256]{1,0:T(1,128)} %bitcast.8, bf16[1024,256]{1,0:T(8,128)(2,1)} %bitcast.6, bf16[256,512]{1,0:T(8,128)(2,1)} %wqk_in.1, bf16[256,256]{1,0:T(8,128)(2,1)} %wv_in.1, bf16[256,256]{1,0:T(8,128)(2,1)} %wout_in.1, ...), custom_call_target="tpu_custom_call" | custom-call | tf_op jit(solution)/shard_map/block/pallas_call | solution.py:350
  51.5 1.9 %copy.11 = bf16[1,1,1024,256]{3,2,1,0:T(8,128)(2,1)} copy(bf16[1,1,1024,256]{3,2,1,0:T(8,128)(2,1)} %bitcast.5) | data formatting | bytes 1048576

commit v4 on v3

--- a/solution.py
+++ b/solution.py
@@ -29,6 +29,11 @@
 DEPTH = 256
 PARTS = 4
 PART = C // PARTS
+HIDDEN = 1024
+MLP_ROWS = 512
+GELU_A = math.sqrt(2 / math.pi)
+GELU_B = GELU_A * 0.044715
+MLP_SPLIT = 4
 ROW_CHUNK = 256
 SCALE = math.log2(math.e) / math.sqrt(HEAD)
 
@@ -40,8 +45,8 @@
 
 
 def kernel(
-    dest, gain_a, gain_m, x_in, wqk_in, wv_in, wout_in, wup_in, wdown_in, out,
-    x_ref, wqk, wv, wout, wup, wdown,
+    x_in, wqk_in, wv_in, wout_in, gain_in, dest_in, out,
+    x_ref, wqk, wv, wout, gain_a, dest,
     normed, settled, near_q, far_q, keys, vals, pool, score, weight, tops, near_sum, near_max, near_t, far_t,
     send, recv, back_send, back_recv,
     out_sems, in_sems, bout_sems, bin_sems, pout_sems, pin_sems, load_sems,
@@ -61,10 +66,10 @@
     loads = [
         pltpu.make_async_copy(source, held, load_sems.at[k])
         for k, (source, held) in enumerate(
-            ((x_in, x_ref), (wqk_in, wqk), (wv_in, wv), (wout_in, wout), (wup_in, wup), (wdown_in, wdown))
+            ((x_in, x_ref), (wqk_in, wqk), (wv_in, wv), (wout_in, wout), (gain_in, gain_a), (dest_in, dest))
         )
     ]
-    for load in loads:
+    for load in loads[::-1]:
         load.start()
     barrier = pltpu.get_barrier_semaphore()
     for d in range(1, LANES):
@@ -73,6 +78,7 @@
         pl.semaphore_signal(barrier, inc=1, device_id=chip_at(d), device_id_type=MESH)
     pl.semaphore_signal(barrier, inc=1, device_id=partner, device_id_type=MESH)
 
+    loads[5].wait()
     offsets = [lax.bitwise_and(lax.shift_right_arithmetic(dest[c], 4) - me, LANES - 1) for c in range(CLUSTERS)]
     first, second, active, upto = [], [], [], []
     count = jnp.int32(0)
@@ -88,30 +94,23 @@
         active.append(hit)
         upto.append(count)
 
+    loads[4].wait()
     loads[0].wait()
 
-    def norm_chunk(i, _):
-        n = norm_rows(x_ref[pl.ds(pl.multiple_of(i * ROW_CHUNK, ROW_CHUNK), ROW_CHUNK), :], gain_a[...])
-        normed[pl.ds(i * (ROW_CHUNK // CLUSTER), ROW_CHUNK // CLUSTER)] = n.reshape(
-            ROW_CHUNK // CLUSTER, CLUSTER, C
-        )
-        return 0
-
-    lax.fori_loop(0, ROWS // ROW_CHUNK, norm_chunk, 0)
+    for c in range(CLUSTERS):
+        normed[c] = norm_rows(x_ref[c * CLUSTER:(c + 1) * CLUSTER, :], gain_a[...])
     for d in range(LANES):
         held = recv if d == 0 else send
         held[2 * d] = normed[first[d]]
         held[2 * d + 1] = normed[second[d]]
 
     pl.semaphore_wait(barrier, LANES - 1 + CHIPS - 1 + 1)
-    sends = []
     for d in range(1, LANES):
         copy = pltpu.make_async_remote_copy(
             src_ref=send.at[pl.ds(2 * d, 2)], dst_ref=recv.at[pl.ds(2 * d, 2)],
-            send_sem=out_sems.at[d], recv_sem=in_sems.at[d], device_id=lane(d), device_id_type=MESH,
+            send_sem=out_sems.at[0], recv_sem=in_sems.at[0], device_id=lane(d), device_id_type=MESH,
         )
         copy.start()
-        sends.append(copy)
 
     def set_keys(rows):
         for h in range(HEADS):
@@ -142,14 +141,12 @@
     pool[:POOLED, :C] = jnp.dot(pooling, key_rows, preferred_element_type=F32).astype(BF)
     value_rows = jnp.dot(normed[...].reshape(ROWS, C), wv[...], preferred_element_type=F32).astype(BF)
     pool[:POOLED, C:] = jnp.dot(pooling, value_rows, preferred_element_type=F32).astype(BF)
-    pooled_sends = []
     for d in range(1, CHIPS):
         copy = pltpu.make_async_remote_copy(
             src_ref=pool.at[pl.ds(0, POOLED)], dst_ref=pool.at[pl.ds(d * POOLED, POOLED)],
-            send_sem=pout_sems.at[d], recv_sem=pin_sems.at[d], device_id=chip_at(d), device_id_type=MESH,
+            send_sem=pout_sems.at[1], recv_sem=pin_sems.at[1], device_id=chip_at(d), device_id_type=MESH,
         )
         copy.start()
-        pooled_sends.append(copy)
 
     def attend(query_t, finish, between=None):
         def spot_of(i):
@@ -260,16 +257,20 @@
 
     attend(near_q, keep)
 
-    for copy in pooled_sends:
-        copy.wait()
+    pltpu.make_async_remote_copy(
+        src_ref=pool.at[pl.ds(POOLED, ROWS // 2 - POOLED)], dst_ref=pool.at[pl.ds(POOLED, ROWS // 2 - POOLED)],
+        send_sem=pout_sems.at[1], recv_sem=pin_sems.at[1], device_id=chip_at(1), device_id_type=MESH,
+    ).wait()
     across = pltpu.make_async_remote_copy(
         src_ref=pool.at[pl.ds(0, ROWS // 2)], dst_ref=pool.at[pl.ds(ROWS // 2, ROWS // 2)],
         send_sem=pout_sems.at[0], recv_sem=pin_sems.at[0], device_id=partner, device_id_type=MESH,
     )
     across.start()
 
-    for copy in sends:
-        copy.wait()
+    pltpu.make_async_remote_copy(
+        src_ref=send.at[pl.ds(2, 2 * LANES - 2)], dst_ref=recv.at[pl.ds(2, 2 * LANES - 2)],
+        send_sem=out_sems.at[0], recv_sem=in_sems.at[0], device_id=lane(1), device_id_type=MESH,
+    ).wait()
     picks = []
     for j in range(LANES // 2):
         d = jnp.int32(0)
@@ -284,7 +285,7 @@
         at = part * LANES + d
         return pltpu.make_async_remote_copy(
             src_ref=back_send.at[at], dst_ref=back_recv.at[at],
-            send_sem=bout_sems.at[at], recv_sem=bin_sems.at[at], device_id=lane(-d), device_id_type=MESH,
+            send_sem=bout_sems.at[part], recv_sem=bin_sems.at[part], device_id=lane(-d), device_id_type=MESH,
         )
 
     def send_back(part):
@@ -304,8 +305,11 @@
     attend(near_q, merge)
 
     for part in range(PARTS):
-        for d in range(1, LANES):
-            back_copy(part, d).wait()
+        rest = pl.ds(part * LANES + 1, LANES - 1)
+        pltpu.make_async_remote_copy(
+            src_ref=back_send.at[rest], dst_ref=back_recv.at[rest],
+            send_sem=bout_sems.at[part], recv_sem=bin_sems.at[part], device_id=lane(1), device_id_type=MESH,
+        ).wait()
     for j in range(LANES // 2):
         block = jnp.concatenate([back_recv[part * LANES + picks[j]] for part in range(PARTS)], axis=0)
         normed[2 * j:2 * j + 2] = block.T.reshape(2, CLUSTER, C)
@@ -317,26 +321,37 @@
         for e in range(c):
             rank = rank + jnp.where(offsets[e] == offsets[c], 1, 0)
         settled[c] = normed[at + jnp.minimum(rank, 1)]
-    for load in loads[3:]:
-        load.wait()
+    loads[3].wait()
 
     def tail(i, _):
         rows = pl.ds(pl.multiple_of(i * ROW_CHUNK, ROW_CHUNK), ROW_CHUNK)
         near = near_t[:, rows].T
         far = settled[pl.ds(i * (ROW_CHUNK // CLUSTER), ROW_CHUNK // CLUSTER)].reshape(ROW_CHUNK, C)
-        after = (
+        out[rows, :] = (
             x_ref[rows, :].astype(F32)
             + jnp.dot(near, wout[...], preferred_element_type=F32)
             + jnp.dot(far, wout[...], preferred_element_type=F32)
         ).astype(BF)
-        mlp_in = norm_rows(after, gain_m[...])
-        hidden = jax.nn.gelu(jnp.dot(mlp_in, wup[...], preferred_element_type=F32), approximate=True).astype(BF)
-        out[rows, :] = (
-            after.astype(F32) + jnp.dot(hidden, wdown[...], preferred_element_type=F32)
-        ).astype(BF)
         return 0
 
     lax.fori_loop(0, ROWS // ROW_CHUNK, tail, 0)
+
+
+def gelu(x):
+    half = 0.5 * x
+    inner = x * (GELU_A + GELU_B * (x * x))
+    return half + half * jnp.tanh(inner)
+
+
+def mlp_kernel(after_ref, gain_m, wup, wdown, out):
+    after = after_ref[...]
+    mlp_in = norm_rows(after, gain_m[...])
+    total = after.astype(F32)
+    for k in range(MLP_SPLIT):
+        cols = pl.ds(k * (HIDDEN // MLP_SPLIT), HIDDEN // MLP_SPLIT)
+        hidden = gelu(jnp.dot(mlp_in, wup[:, cols], preferred_element_type=F32)).astype(BF)
+        total = total + jnp.dot(hidden, wdown[cols, :], preferred_element_type=F32)
+    out[...] = total.astype(BF)
 
 
 def per_device(points, gain_attn, w_query_key, w_value, w_out, gain_mlp, w_up, w_down, cluster_dest):
@@ -345,14 +360,16 @@
     slots = pltpu.VMEM((2 * LANES, CLUSTER, C), BF)
     turned = pltpu.VMEM((C, ROWS), BF)
     parts = pltpu.VMEM((PARTS * LANES, PART, 2 * CLUSTER), BF)
-    anywhere = pl.BlockSpec(memory_space=pl.ANY)
-    moved = (points.reshape(ROWS, C), w_query_key, w_value, w_out, w_up, w_down)
-    result = pl.pallas_call(
+    anywhere = pl.BlockSpec(memory_space=pltpu.HBM)
+    moved = (points.reshape(ROWS, C), w_query_key, w_value, w_out, gain_attn.reshape(1, C), cluster_dest.reshape(CLUSTERS))
+    moved = tuple(pltpu.with_memory_space_constraint(a, pltpu.HBM) for a in moved)
+    after = pl.pallas_call(
         kernel,
         out_shape=jax.ShapeDtypeStruct((ROWS, C), BF),
-        in_specs=[pl.BlockSpec(memory_space=pltpu.SMEM)] + [vmem] * 2 + [anywhere] * 6,
+        in_specs=[anywhere] * 6,
         out_specs=vmem,
-        scratch_shapes=[pltpu.VMEM(a.shape, BF) for a in moved]
+        scratch_shapes=[pltpu.VMEM(a.shape, a.dtype) for a in moved[:-1]]
+        + [pltpu.SMEM((CLUSTERS,), jnp.int32)]
         + [
             clusters, clusters,
             turned, turned,
@@ -368,16 +385,27 @@
             pltpu.VMEM((PARTS * LANES // 2, PART, 2 * CLUSTER), BF),
             slots, slots, parts, parts,
         ]
-        + [pltpu.SemaphoreType.DMA((LANES,))] * 2
-        + [pltpu.SemaphoreType.DMA((PARTS * LANES,))] * 2
-        + [pltpu.SemaphoreType.DMA((CHIPS,))] * 3,
+        + [pltpu.SemaphoreType.DMA((1,))] * 2
+        + [pltpu.SemaphoreType.DMA((PARTS,))] * 2
+        + [pltpu.SemaphoreType.DMA((2,))] * 2
+        + [pltpu.SemaphoreType.DMA((6,))],
         compiler_params=pltpu.CompilerParams(
-            collective_id=0, has_side_effects=True, vmem_limit_bytes=60 * 1024 * 1024
+            collective_id=0, has_side_effects=True, vmem_limit_bytes=40 * 1024 * 1024
         ),
         name="block",
     )(
-        cluster_dest.reshape(CLUSTERS), gain_attn.reshape(1, C), gain_mlp.reshape(1, C), *moved
+        *moved
     )
+    rows = pl.BlockSpec((MLP_ROWS, C), lambda i: (i, 0))
+    result = pl.pallas_call(
+        mlp_kernel,
+        grid=(ROWS // MLP_ROWS,),
+        out_shape=jax.ShapeDtypeStruct((ROWS, C), BF),
+        in_specs=[rows] + [vmem] * 3,
+        out_specs=rows,
+        compiler_params=pltpu.CompilerParams(vmem_limit_bytes=12 * 1024 * 1024),
+        name="mlp",
+    )(after, gain_mlp.reshape(1, C), w_up, w_down)
     return result.reshape(points.shape)
 
 

time: 53.5 us -> 48.2 us (0.901)
  Pallas kernels: 51.4 us -> 48 us
  local copies, waits for them, and re-layouts: 1.87 us -> 0.01 us
    pallas_call x1, Pallas kernels: 51.4 us -> 45.4 us  [per_device(): pl.pallas_call(kernel, out_shape=jax.ShapeDtypeStruct((ROWS, C), BF), in_...]
    pallas_call x0 -> x1, Pallas kernels: none -> 2.63 us  [per_device(): pl.pallas_call(mlp_kernel, grid=(ROWS // MLP_ROWS,), out_shape=jax.ShapeD...]
    unnamed x1 -> x6, local copies, waits for them, and re-layouts: 1.87 us -> 0.01 us
where the time goes in v4:
time: 48.2 us; the launch traced here: 48.1 us
  Pallas kernels  48 us (100%)
    pallas_call x1, Pallas kernels, per_device(): pl.pallas_call(kernel, out_shape=jax.ShapeDtypeStruct((ROWS, C), BF), in_...  45.4 us
    pallas_call x1, Pallas kernels, per_device(): pl.pallas_call(mlp_kernel, grid=(ROWS // MLP_ROWS,), out_shape=jax.ShapeD...  2.63 us

profile of v4, /device:TPU:8, one launch (start us, length us, event | category | flops | bytes accessed | tf_op | source)
XLA Modules:
  0.0 48.1 jit_solution(17251862851417000871)
XLA Ops:
  0.0 0.0 copy-start
  0.0 0.0 copy-start.1
  0.0 0.0 copy-start.2
  0.0 45.4 %block.1.after_ref = bf16[1024,256]{1,0:T(8,128)(2,1)S(1)} custom-call(bf16[1024,256]{1,0:T(8,128)(2,1)} %bitcast.6, bf16[256,512]{1,0:T(8,128)(2,1)} %wqk_in.1, bf16[256,256]{1,0:T(8,128)(2,1)} %wv_in.1, bf16[256,256]{1,0:T(8,128)(2,1)} %wout_in.1, f32[1,256]{1,0:T(1,128)} %bitcast.7, s32[16]{0:T(128)} %bitcast.8), custom_call_target="tpu_custom_call" | custom-call | tf_op jit(solution)/shard_map/block/pallas_call | solution.py:366
  45.4 0.0 copy-done
  45.4 0.0 copy-done.1
  45.4 0.0 copy-done.2
  45.4 2.6 %mlp.1 = bf16[1024,256]{1,0:T(8,128)(2,1)} custom-call(bf16[1024,256]{1,0:T(8,128)(2,1)S(1)} %block.1.after_ref, f32[1,256]{1,0:T(1,128)S(1)} %bitcast.5, bf16[256,1024]{1,0:T(8,128)(2,1)S(1)} %copy-done, bf16[1024,256]{1,0:T(8,128)(2,1)S(1)} %copy-done.1), custom_call_target="tpu_custom_call" | custom-call | tf_op jit(solution)/shard_map/mlp/pallas_call | solution.py:400
Async XLA Ops:
  0.0 45.4 %copy-start = (bf16[256,1024]{1,0:T(8,128)(2,1)S(1)}, bf16[256,1024]{1,0:T(8,128)(2,1)}, u32[]{:S(2)}) copy-start(bf16[256,1024]{1,0:T(8,128)(2,1)} %wup.1) | copy-start | bytes 1572868
  0.0 45.4 %copy-start.1 = (bf16[1024,256]{1,0:T(8,128)(2,1)S(1)}, bf16[1024,256]{1,0:T(8,128)(2,1)}, u32[]{:S(2)}) copy-start(bf16[1024,256]{1,0:T(8,128)(2,1)} %wdown.1) | copy-start | bytes 1572868
  0.0 45.4 %copy-start.2 = (f32[256]{0:T(256)S(1)}, f32[256]{0:T(256)}, u32[]{:S(2)}) copy-start(f32[256]{0:T(256)} %param.14) | copy-start | bytes 3076

commit v5 on v4

--- a/solution.py
+++ b/solution.py
@@ -47,7 +47,7 @@
 def kernel(
     x_in, wqk_in, wv_in, wout_in, gain_in, dest_in, out,
     x_ref, wqk, wv, wout, gain_a, dest,
-    normed, settled, near_q, far_q, keys, vals, pool, score, weight, tops, near_sum, near_max, near_t, far_t,
+    normed, settled, near_q, far_q, keys, vals, pool_keys, pool_vals, pool, score, weight, tops, near_sum, near_max, near_t, far_t,
     send, recv, back_send, back_recv,
     out_sems, in_sems, bout_sems, bin_sems, pout_sems, pin_sems, load_sems,
 ):
@@ -112,13 +112,18 @@
         )
         copy.start()
 
+    def head_cols(rows, h):
+        start = h % 4 * HEAD
+        half = rows[:, h // 4 * 128:(h // 4 + 1) * 128]
+        return (pltpu.roll(half, 128 - start, axis=1) if start else half)[:, :HEAD]
+
     def set_keys(rows):
         for h in range(HEADS):
-            keys[h] = rows[:, h * HEAD:(h + 1) * HEAD]
-
-    def set_values(value_t):
-        for h in range(HEADS):
-            vals[h, :HEAD, :] = value_t[h * HEAD:(h + 1) * HEAD, :]
+            keys[h] = head_cols(rows, h)
+
+    def set_values(held, value_t, first_head=0):
+        for h in range(value_t.shape[0] // HEAD):
+            held[first_head + h, :HEAD, :] = value_t[h * HEAD:(h + 1) * HEAD, :]
 
     def project(source, query_t):
         states = source[...].reshape(ROWS, C)
@@ -126,11 +131,12 @@
         query_t[...] = jnp.dot(wqk[:, :C].T, turned, preferred_element_type=F32).astype(BF)
         key_rows = jnp.dot(states, wqk[:, C:], preferred_element_type=F32).astype(BF)
         set_keys(key_rows)
-        set_values(jnp.dot(wv[...].T, turned, preferred_element_type=F32).astype(BF))
+        set_values(vals, jnp.dot(wv[...].T, turned, preferred_element_type=F32).astype(BF))
         return key_rows
 
     for h in range(HEADS):
         vals[h, HEAD:, :] = jnp.ones((16, ROWS), BF)
+        pool_vals[h, HEAD:, :] = jnp.ones((16, ROWS), BF)
     for load in loads[1:3]:
         load.wait()
     key_rows = project(normed, near_q)
@@ -148,14 +154,14 @@
         )
         copy.start()
 
-    def attend(query_t, finish, between=None):
+    def attend(query_t, keys, vals, finish, between=None, ready=False, following=None, before_last=None, side=None):
         def spot_of(i):
             return i // QBLOCKS, pl.ds(pl.multiple_of(i % QBLOCKS * QB, QB), QB)
 
         def head_rows(h):
             return pl.ds(pl.multiple_of(h * HEAD, HEAD), HEAD)
 
-        def scores_of(i, slot, r, top):
+        def scores_of(i, slot, r, top, query_t=query_t, keys=keys):
             h, cols = spot_of(i)
             rows = pl.ds(r * PIECE, PIECE)
             s = jnp.dot(keys[h, rows, :], query_t[head_rows(h), cols], preferred_element_type=F32)
@@ -190,6 +196,11 @@
                     rows = pl.ds(r * PIECE, PIECE)
                     if not last:
                         new_top = scores_of(new, other, r, new_top)
+                    else:
+                        if side is not None:
+                            side(b * (ROWS // PIECE) + r)
+                        if following is not None:
+                            new_top = scores_of(b, other, r, new_top, *following)
                     weight[now, rows, :] = jnp.exp2((score[now, rows, :] - top) * SCALE).astype(BF)
                     if (r + 1) * PIECE % DEPTH == 0:
                         part = (r + 1) * PIECE // DEPTH - 1
@@ -199,10 +210,10 @@
                 finish(old_head, old_cols, old_top, total)
                 if last:
                     finish(head, cols, top, last_total)
-                else:
+                if not last or following is not None:
                     tops[other] = new_top
 
-        for b in range(GROUP):
+        for b in range(0 if ready else GROUP):
             top = low
             for r in range(ROWS // PIECE):
                 top = scores_of(b, b, r, top)
@@ -223,6 +234,9 @@
             @pl.when(t < pairs - 1)
             def _():
                 step(2 * t + 1, False)
+
+            if before_last is not None:
+                pl.when(t == pairs - 1)(before_last)
 
             @pl.when(t == pairs - 1)
             def _():
@@ -255,7 +269,7 @@
             at = h // 2 * (LANES // 2) + cols.start // (2 * CLUSTER) + k
             far_t[at, rows, :] = block[:, k * 2 * CLUSTER:(k + 1) * 2 * CLUSTER]
 
-    attend(near_q, keep)
+    attend(near_q, keys, vals, keep)
 
     pltpu.make_async_remote_copy(
         src_ref=pool.at[pl.ds(POOLED, ROWS // 2 - POOLED)], dst_ref=pool.at[pl.ds(POOLED, ROWS // 2 - POOLED)],
@@ -296,23 +310,37 @@
         for d in range(1, LANES):
             back_copy(part, d).start()
 
-    attend(far_q, far_done, send_back)
+    def pooled_here():
+        across.wait()
+        pool_keys[0] = head_cols(pool, 0)
+
+    def pooled_layout(k):
+        if 1 <= k < HEADS:
+            pool_keys[k] = head_cols(pool, k)
+        elif k in (HEADS, HEADS + 4):
+            first_head = k - HEADS
+            set_values(pool_vals, pool[:, C + first_head * HEAD:C + (first_head + 4) * HEAD].T, first_head)
+
+    attend(
+        far_q, keys, vals, far_done, send_back,
+        following=(near_q, pool_keys), before_last=pooled_here, side=pooled_layout,
+    )
     send_back(PARTS - 1)
 
-    across.wait()
-    set_keys(pool[:, :C])
-    set_values(pool[:, C:].T)
-    attend(near_q, merge)
-
-    for part in range(PARTS):
-        rest = pl.ds(part * LANES + 1, LANES - 1)
-        pltpu.make_async_remote_copy(
-            src_ref=back_send.at[rest], dst_ref=back_recv.at[rest],
-            send_sem=bout_sems.at[part], recv_sem=bin_sems.at[part], device_id=lane(1), device_id_type=MESH,
-        ).wait()
-    for j in range(LANES // 2):
-        block = jnp.concatenate([back_recv[part * LANES + picks[j]] for part in range(PARTS)], axis=0)
-        normed[2 * j:2 * j + 2] = block.T.reshape(2, CLUSTER, C)
+    def returned():
+        for part in range(PARTS):
+            rest = pl.ds(part * LANES + 1, LANES - 1)
+            pltpu.make_async_remote_copy(
+                src_ref=back_send.at[rest], dst_ref=back_recv.at[rest],
+                send_sem=bout_sems.at[part], recv_sem=bin_sems.at[part], device_id=lane(1), device_id_type=MESH,
+            ).wait()
+
+    def turn_back(k):
+        if k < LANES // 2:
+            block = jnp.concatenate([back_recv[part * LANES + picks[k]] for part in range(PARTS)], axis=0)
+            normed[2 * k:2 * k + 2] = block.T.reshape(2, CLUSTER, C)
+
+    attend(near_q, pool_keys, pool_vals, merge, ready=True, before_last=returned, side=turn_back)
     for c in range(CLUSTERS):
         at = jnp.int32(0)
         for j in range(LANES // 2 - 1):
@@ -373,6 +401,8 @@
         + [
             clusters, clusters,
             turned, turned,
+            pltpu.VMEM((HEADS, ROWS, HEAD), BF),
+            pltpu.VMEM((HEADS, 48, ROWS), BF),
             pltpu.VMEM((HEADS, ROWS, HEAD), BF),
             pltpu.VMEM((HEADS, 48, ROWS), BF),
             pltpu.VMEM((ROWS, 2 * C), BF),

time: 48.2 us -> 47.9 us (level)
  the two profiles are of different devices: /device:TPU:8 before, /device:TPU:1 now
where the time goes in v5:
time: 47.9 us; the launch traced here: 47.8 us
  Pallas kernels  47.7 us (100%)
    pallas_call x1, Pallas kernels, per_device(): pl.pallas_call(kernel, out_shape=jax.ShapeDtypeStruct((ROWS, C), BF), in_...  45.1 us
    pallas_call x1, Pallas kernels, per_device(): pl.pallas_call(mlp_kernel, grid=(ROWS // MLP_ROWS,), out_shape=jax.ShapeD...  2.63 us

profile of v5, /device:TPU:1, one launch (start us, length us, event | category | flops | bytes accessed | tf_op | source)
XLA Modules:
  0.0 47.8 jit_solution(1409904771119711954)
XLA Ops:
  0.0 0.0 copy-start
  0.0 0.0 copy-start.1
  0.0 0.0 copy-start.2
  0.0 45.1 %block.1.after_ref = bf16[1024,256]{1,0:T(8,128)(2,1)S(1)} custom-call(bf16[1024,256]{1,0:T(8,128)(2,1)} %bitcast.6, bf16[256,512]{1,0:T(8,128)(2,1)} %wqk_in.1, bf16[256,256]{1,0:T(8,128)(2,1)} %wv_in.1, bf16[256,256]{1,0:T(8,128)(2,1)} %wout_in.1, f32[1,256]{1,0:T(1,128)} %bitcast.7, s32[16]{0:T(128)} %bitcast.8), custom_call_target="tpu_custom_call" | custom-call | tf_op jit(solution)/shard_map/block/pallas_call | solution.py:394
  45.1 0.0 copy-done
  45.1 0.0 copy-done.1
  45.1 0.0 copy-done.2
  45.1 2.6 %mlp.1 = bf16[1024,256]{1,0:T(8,128)(2,1)} custom-call(bf16[1024,256]{1,0:T(8,128)(2,1)S(1)} %block.1.after_ref, f32[1,256]{1,0:T(1,128)S(1)} %bitcast.5, bf16[256,1024]{1,0:T(8,128)(2,1)S(1)} %copy-done, bf16[1024,256]{1,0:T(8,128)(2,1)S(1)} %copy-done.1), custom_call_target="tpu_custom_call" | custom-call | tf_op jit(solution)/shard_map/mlp/pallas_call | solution.py:430
Async XLA Ops:
  0.0 45.1 %copy-start = (bf16[256,1024]{1,0:T(8,128)(2,1)S(1)}, bf16[256,1024]{1,0:T(8,128)(2,1)}, u32[]{:S(2)}) copy-start(bf16[256,1024]{1,0:T(8,128)(2,1)} %wup.1) | copy-start | bytes 1572868
  0.0 45.1 %copy-start.1 = (bf16[1024,256]{1,0:T(8,128)(2,1)S(1)}, bf16[1024,256]{1,0:T(8,128)(2,1)}, u32[]{:S(2)}) copy-start(bf16[1024,256]{1,0:T(8,128)(2,1)} %wdown.1) | copy-start | bytes 1572868
  0.0 45.1 %copy-start.2 = (f32[256]{0:T(256)S(1)}, f32[256]{0:T(256)}, u32[]{:S(2)}) copy-start(f32[256]{0:T(256)} %param.14) | copy-start | bytes 3076

commit v6 on v5

--- a/solution.py
+++ b/solution.py
@@ -69,8 +69,8 @@
             ((x_in, x_ref), (wqk_in, wqk), (wv_in, wv), (wout_in, wout), (gain_in, gain_a), (dest_in, dest))
         )
     ]
-    for load in loads[::-1]:
-        load.start()
+    for k in (5, 4, 0, 1, 2, 3):
+        loads[k].start()
     barrier = pltpu.get_barrier_semaphore()
     for d in range(1, LANES):
         pl.semaphore_signal(barrier, inc=1, device_id=lane(d), device_id_type=MESH)
@@ -83,6 +83,9 @@
     first, second, active, upto = [], [], [], []
     count = jnp.int32(0)
     for d in range(LANES):
+        if d == LANES // 2:
+            loads[4].wait()
+            loads[0].wait()
         lo, hi = jnp.int32(CLUSTERS), jnp.int32(0)
         for c in range(CLUSTERS):
             hi = jnp.where(offsets[c] == d, c, hi)
@@ -94,8 +97,6 @@
         active.append(hit)
         upto.append(count)
 
-    loads[4].wait()
-    loads[0].wait()
 
     for c in range(CLUSTERS):
         normed[c] = norm_rows(x_ref[c * CLUSTER:(c + 1) * CLUSTER, :], gain_a[...])
@@ -281,19 +282,20 @@
     )
     across.start()
 
-    pltpu.make_async_remote_copy(
-        src_ref=send.at[pl.ds(2, 2 * LANES - 2)], dst_ref=recv.at[pl.ds(2, 2 * LANES - 2)],
-        send_sem=out_sems.at[0], recv_sem=in_sems.at[0], device_id=lane(1), device_id_type=MESH,
-    ).wait()
     picks = []
     for j in range(LANES // 2):
         d = jnp.int32(0)
         for k in range(LANES):
             d = d + jnp.where(upto[k] <= j, 1, 0)
-        d = jnp.minimum(d, LANES - 1)
-        picks.append(d)
-        settled[2 * j] = recv[2 * d]
-        settled[2 * j + 1] = recv[2 * d + 1]
+        picks.append(jnp.minimum(d, LANES - 1))
+
+    pltpu.make_async_remote_copy(
+        src_ref=send.at[pl.ds(2, 2 * LANES - 2)], dst_ref=recv.at[pl.ds(2, 2 * LANES - 2)],
+        send_sem=out_sems.at[0], recv_sem=in_sems.at[0], device_id=lane(1), device_id_type=MESH,
+    ).wait()
+    for j in range(LANES // 2):
+        settled[2 * j] = recv[2 * picks[j]]
+        settled[2 * j + 1] = recv[2 * picks[j] + 1]
     project(settled, far_q)
     def back_copy(part, d):
         at = part * LANES + d
@@ -341,28 +343,24 @@
             normed[2 * k:2 * k + 2] = block.T.reshape(2, CLUSTER, C)
 
     attend(near_q, pool_keys, pool_vals, merge, ready=True, before_last=returned, side=turn_back)
-    for c in range(CLUSTERS):
-        at = jnp.int32(0)
-        for j in range(LANES // 2 - 1):
-            at = at + jnp.where(picks[j] < offsets[c], 2, 0)
-        rank = jnp.int32(0)
-        for e in range(c):
-            rank = rank + jnp.where(offsets[e] == offsets[c], 1, 0)
-        settled[c] = normed[at + jnp.minimum(rank, 1)]
     loads[3].wait()
-
-    def tail(i, _):
-        rows = pl.ds(pl.multiple_of(i * ROW_CHUNK, ROW_CHUNK), ROW_CHUNK)
-        near = near_t[:, rows].T
-        far = settled[pl.ds(i * (ROW_CHUNK // CLUSTER), ROW_CHUNK // CLUSTER)].reshape(ROW_CHUNK, C)
+    for i in range(ROWS // ROW_CHUNK):
+        rows = slice(i * ROW_CHUNK, (i + 1) * ROW_CHUNK)
+        per_chunk = ROW_CHUNK // CLUSTER
+        for c in range(i * per_chunk, (i + 1) * per_chunk):
+            at = jnp.int32(0)
+            for j in range(LANES // 2 - 1):
+                at = at + jnp.where(picks[j] < offsets[c], 2, 0)
+            rank = jnp.int32(0)
+            for e in range(c):
+                rank = rank + jnp.where(offsets[e] == offsets[c], 1, 0)
+            settled[c] = normed[at + jnp.minimum(rank, 1)]
+        far = settled[i * per_chunk:(i + 1) * per_chunk].reshape(ROW_CHUNK, C)
         out[rows, :] = (
             x_ref[rows, :].astype(F32)
-            + jnp.dot(near, wout[...], preferred_element_type=F32)
+            + jnp.dot(near_t[:, rows].T, wout[...], preferred_element_type=F32)
             + jnp.dot(far, wout[...], preferred_element_type=F32)
         ).astype(BF)
-        return 0
-
-    lax.fori_loop(0, ROWS // ROW_CHUNK, tail, 0)
 
 
 def gelu(x):

time: 47.9 us -> 47.1 us (0.983)
  Pallas kernels: 47.7 us -> 46.9 us
    pallas_call x1, Pallas kernels: 45.1 us -> 44.3 us  [per_device(): pl.pallas_call(kernel, out_shape=jax.ShapeDtypeStruct((ROWS, C), BF), in_...]
where the time goes in v6:
time: 47.1 us; the launch traced here: 47 us
  Pallas kernels  46.9 us (100%)
    pallas_call x1, Pallas kernels, per_device(): pl.pallas_call(kernel, out_shape=jax.ShapeDtypeStruct((ROWS, C), BF), in_...  44.3 us
    pallas_call x1, Pallas kernels, per_device(): pl.pallas_call(mlp_kernel, grid=(ROWS // MLP_ROWS,), out_shape=jax.ShapeD...  2.63 us

profile of v6, /device:TPU:1, one launch (start us, length us, event | category | flops | bytes accessed | tf_op | source)
XLA Modules:
  0.0 47.0 jit_solution(7468473892743525834)
XLA Ops:
  0.0 0.0 copy-start
  0.0 0.0 copy-start.1
  0.0 0.0 copy-start.2
  0.0 44.3 %block.1.after_ref = bf16[1024,256]{1,0:T(8,128)(2,1)S(1)} custom-call(bf16[1024,256]{1,0:T(8,128)(2,1)} %bitcast.6, bf16[256,512]{1,0:T(8,128)(2,1)} %wqk_in.1, bf16[256,256]{1,0:T(8,128)(2,1)} %wv_in.1, bf16[256,256]{1,0:T(8,128)(2,1)} %wout_in.1, f32[1,256]{1,0:T(1,128)} %bitcast.7, s32[16]{0:T(128)} %bitcast.8), custom_call_target="tpu_custom_call" | custom-call | tf_op jit(solution)/shard_map/block/pallas_call | solution.py:392
  44.3 0.0 copy-done
  44.3 0.0 copy-done.1
  44.3 0.0 copy-done.2
  44.3 2.6 %mlp.1 = bf16[1024,256]{1,0:T(8,128)(2,1)} custom-call(bf16[1024,256]{1,0:T(8,128)(2,1)S(1)} %block.1.after_ref, f32[1,256]{1,0:T(1,128)S(1)} %bitcast.5, bf16[256,1024]{1,0:T(8,128)(2,1)S(1)} %copy-done, bf16[1024,256]{1,0:T(8,128)(2,1)S(1)} %copy-done.1), custom_call_target="tpu_custom_call" | custom-call | tf_op jit(solution)/shard_map/mlp/pallas_call | solution.py:428
Async XLA Ops:
  0.0 44.3 %copy-start = (bf16[256,1024]{1,0:T(8,128)(2,1)S(1)}, bf16[256,1024]{1,0:T(8,128)(2,1)}, u32[]{:S(2)}) copy-start(bf16[256,1024]{1,0:T(8,128)(2,1)} %wup.1) | copy-start | bytes 1572868
  0.0 44.3 %copy-start.1 = (bf16[1024,256]{1,0:T(8,128)(2,1)S(1)}, bf16[1024,256]{1,0:T(8,128)(2,1)}, u32[]{:S(2)}) copy-start(bf16[1024,256]{1,0:T(8,128)(2,1)} %wdown.1) | copy-start | bytes 1572868
  0.0 44.3 %copy-start.2 = (f32[256]{0:T(256)S(1)}, f32[256]{0:T(256)}, u32[]{:S(2)}) copy-start(f32[256]{0:T(256)} %param.14) | copy-start | bytes 3076

commit v7 on v6

--- a/solution.py
+++ b/solution.py
@@ -21,6 +21,8 @@
 POOL = 16
 POOLED = ROWS // POOL
 CHIPS = 8
+FAR_FIRST = (10, 9, 11, 6, 14, 5, 7, 13, 15, 2, 8, 1, 3, 4, 12)
+CHIPS_FAR_FIRST = (4, 3, 5, 2, 6, 1, 7)
 QB = 512
 QBLOCKS = ROWS // QB
 BLOCKS = HEADS * QBLOCKS
@@ -72,9 +74,12 @@
     for k in (5, 4, 0, 1, 2, 3):
         loads[k].start()
     barrier = pltpu.get_barrier_semaphore()
-    for d in range(1, LANES):
+    pl.semaphore_signal(barrier, inc=1, device_id=lane(FAR_FIRST[0]), device_id_type=MESH)
+    for d in CHIPS_FAR_FIRST[:3]:
+        pl.semaphore_signal(barrier, inc=1, device_id=chip_at(d), device_id_type=MESH)
+    for d in FAR_FIRST[1:]:
         pl.semaphore_signal(barrier, inc=1, device_id=lane(d), device_id_type=MESH)
-    for d in range(1, CHIPS):
+    for d in CHIPS_FAR_FIRST[3:]:
         pl.semaphore_signal(barrier, inc=1, device_id=chip_at(d), device_id_type=MESH)
     pl.semaphore_signal(barrier, inc=1, device_id=partner, device_id_type=MESH)
 
@@ -106,7 +111,7 @@
         held[2 * d + 1] = normed[second[d]]
 
     pl.semaphore_wait(barrier, LANES - 1 + CHIPS - 1 + 1)
-    for d in range(1, LANES):
+    for d in FAR_FIRST:
         copy = pltpu.make_async_remote_copy(
             src_ref=send.at[pl.ds(2 * d, 2)], dst_ref=recv.at[pl.ds(2 * d, 2)],
             send_sem=out_sems.at[0], recv_sem=in_sems.at[0], device_id=lane(d), device_id_type=MESH,
@@ -148,7 +153,7 @@
     pool[:POOLED, :C] = jnp.dot(pooling, key_rows, preferred_element_type=F32).astype(BF)
     value_rows = jnp.dot(normed[...].reshape(ROWS, C), wv[...], preferred_element_type=F32).astype(BF)
     pool[:POOLED, C:] = jnp.dot(pooling, value_rows, preferred_element_type=F32).astype(BF)
-    for d in range(1, CHIPS):
+    for d in CHIPS_FAR_FIRST:
         copy = pltpu.make_async_remote_copy(
             src_ref=pool.at[pl.ds(0, POOLED)], dst_ref=pool.at[pl.ds(d * POOLED, POOLED)],
             send_sem=pout_sems.at[1], recv_sem=pin_sems.at[1], device_id=chip_at(d), device_id_type=MESH,
@@ -309,7 +314,7 @@
             held = back_recv if d == 0 else back_send
             j = jnp.minimum(upto[d] - active[d], LANES // 2 - 1)
             held[part * LANES + d] = far_t[part * (LANES // 2) + j]
-        for d in range(1, LANES):
+        for d in FAR_FIRST:
             back_copy(part, d).start()
 
     def pooled_here():

time: 47.1 us -> 46.9 us (level)
  no operation moved by 1% of the time
where the time goes in v7:
time: 46.9 us; the launch traced here: 46.8 us
  Pallas kernels  46.8 us (100%)
    pallas_call x1, Pallas kernels, per_device(): pl.pallas_call(kernel, out_shape=jax.ShapeDtypeStruct((ROWS, C), BF), in_...  44.2 us
    pallas_call x1, Pallas kernels, per_device(): pl.pallas_call(mlp_kernel, grid=(ROWS // MLP_ROWS,), out_shape=jax.ShapeD...  2.63 us

profile of v7, /device:TPU:1, one launch (start us, length us, event | category | flops | bytes accessed | tf_op | source)
XLA Modules:
  0.0 46.8 jit_solution(3111588664274829511)
XLA Ops:
  0.0 0.0 copy-start
  0.0 0.0 copy-start.1
  0.0 0.0 copy-start.2
  0.0 44.2 %block.1.after_ref = bf16[1024,256]{1,0:T(8,128)(2,1)S(1)} custom-call(bf16[1024,256]{1,0:T(8,128)(2,1)} %bitcast.6, bf16[256,512]{1,0:T(8,128)(2,1)} %wqk_in.1, bf16[256,256]{1,0:T(8,128)(2,1)} %wv_in.1, bf16[256,256]{1,0:T(8,128)(2,1)} %wout_in.1, f32[1,256]{1,0:T(1,128)} %bitcast.7, s32[16]{0:T(128)} %bitcast.8), custom_call_target="tpu_custom_call" | custom-call | tf_op jit(solution)/shard_map/block/pallas_call | solution.py:397
  44.2 0.0 copy-done
  44.2 0.0 copy-done.1
  44.2 0.0 copy-done.2
  44.2 2.6 %mlp.1 = bf16[1024,256]{1,0:T(8,128)(2,1)} custom-call(bf16[1024,256]{1,0:T(8,128)(2,1)S(1)} %block.1.after_ref, f32[1,256]{1,0:T(1,128)S(1)} %bitcast.5, bf16[256,1024]{1,0:T(8,128)(2,1)S(1)} %copy-done, bf16[1024,256]{1,0:T(8,128)(2,1)S(1)} %copy-done.1), custom_call_target="tpu_custom_call" | custom-call | tf_op jit(solution)/shard_map/mlp/pallas_call | solution.py:433
Async XLA Ops:
  0.0 44.2 %copy-start = (bf16[256,1024]{1,0:T(8,128)(2,1)S(1)}, bf16[256,1024]{1,0:T(8,128)(2,1)}, u32[]{:S(2)}) copy-start(bf16[256,1024]{1,0:T(8,128)(2,1)} %wup.1) | copy-start | bytes 1572868
  0.0 44.2 %copy-start.1 = (bf16[1024,256]{1,0:T(8,128)(2,1)S(1)}, bf16[1024,256]{1,0:T(8,128)(2,1)}, u32[]{:S(2)}) copy-start(bf16[1024,256]{1,0:T(8,128)(2,1)} %wdown.1) | copy-start | bytes 1572868
  0.0 44.2 %copy-start.2 = (f32[256]{0:T(256)S(1)}, f32[256]{0:T(256)}, u32[]{:S(2)}) copy-start(f32[256]{0:T(256)} %param.14) | copy-start | bytes 3076

commit v8 on v7

--- a/solution.py
+++ b/solution.py
@@ -32,7 +32,7 @@
 PARTS = 4
 PART = C // PARTS
 HIDDEN = 1024
-MLP_ROWS = 512
+MLP_ROWS = 1024
 GELU_A = math.sqrt(2 / math.pi)
 GELU_B = GELU_A * 0.044715
 MLP_SPLIT = 4

time: 46.9 us -> 46.7 us (level)
  no operation moved by 1% of the time
where the time goes in v8:
time: 46.7 us; the launch traced here: 46.6 us
  Pallas kernels  46.6 us (100%)
    pallas_call x1, Pallas kernels, per_device(): pl.pallas_call(kernel, out_shape=jax.ShapeDtypeStruct((ROWS, C), BF), in_...  44.2 us
    pallas_call x1, Pallas kernels, per_device(): pl.pallas_call(mlp_kernel, grid=(ROWS // MLP_ROWS,), out_shape=jax.ShapeD...  2.42 us

profile of v8, /device:TPU:1, one launch (start us, length us, event | category | flops | bytes accessed | tf_op | source)
XLA Modules:
  0.0 46.6 jit_solution(14364183464219952096)
XLA Ops:
  0.0 0.0 copy-start
  0.0 0.0 copy-start.1
  0.0 0.0 copy-start.2
  0.0 44.2 %block.1.after_ref = bf16[1024,256]{1,0:T(8,128)(2,1)S(1)} custom-call(bf16[1024,256]{1,0:T(8,128)(2,1)} %bitcast.6, bf16[256,512]{1,0:T(8,128)(2,1)} %wqk_in.1, bf16[256,256]{1,0:T(8,128)(2,1)} %wv_in.1, bf16[256,256]{1,0:T(8,128)(2,1)} %wout_in.1, f32[1,256]{1,0:T(1,128)} %bitcast.7, s32[16]{0:T(128)} %bitcast.8), custom_call_target="tpu_custom_call" | custom-call | tf_op jit(solution)/shard_map/block/pallas_call | solution.py:397
  44.2 0.0 copy-done
  44.2 0.0 copy-done.1
  44.2 0.0 copy-done.2
  44.2 2.4 %mlp.1 = bf16[1024,256]{1,0:T(8,128)(2,1)} custom-call(bf16[1024,256]{1,0:T(8,128)(2,1)S(1)} %block.1.after_ref, f32[1,256]{1,0:T(1,128)S(1)} %bitcast.5, bf16[256,1024]{1,0:T(8,128)(2,1)S(1)} %copy-done, bf16[1024,256]{1,0:T(8,128)(2,1)S(1)} %copy-done.1), custom_call_target="tpu_custom_call" | custom-call | tf_op jit(solution)/shard_map/mlp/pallas_call | solution.py:433
Async XLA Ops:
  0.0 44.2 %copy-start = (bf16[256,1024]{1,0:T(8,128)(2,1)S(1)}, bf16[256,1024]{1,0:T(8,128)(2,1)}, u32[]{:S(2)}) copy-start(bf16[256,1024]{1,0:T(8,128)(2,1)} %wup.1) | copy-start | bytes 1572868
  0.0 44.2 %copy-start.1 = (bf16[1024,256]{1,0:T(8,128)(2,1)S(1)}, bf16[1024,256]{1,0:T(8,128)(2,1)}, u32[]{:S(2)}) copy-start(bf16[1024,256]{1,0:T(8,128)(2,1)} %wdown.1) | copy-start | bytes 1572868
  0.0 44.2 %copy-start.2 = (f32[256]{0:T(256)S(1)}, f32[256]{0:T(256)}, u32[]{:S(2)}) copy-start(f32[256]{0:T(256)} %param.14) | copy-start | bytes 3076
